TPU v7x, 256 devices: a whole 4x4x8 slice. The times are simulated.
256 devices in a mesh: wave: 32 (over z, x_lo, core), depth: 8 (over x_hi, y).
Axes of the slice: x: 4 (x_hi: 2, x_lo: 2; x = x_hi * 2 + x_lo), y: 4, z: 8, core: 2. Of those that a mesh axis runs over, the one named last changes fastest.
Arguments:
- slip_field: bfloat16 [16, 2, 1024, 1024], P('depth', None, 'wave'), may hold values from -6 to 6
- slip_mask: int32 [16, 32, 32], P('depth', 'wave'), may hold values 0 or 1
- slice_layer: int32 [64], replicated, may hold values from 0 to 15, as said below
- layer_material: int32 [16], replicated, may hold values from 0 to 7
- materials: float32 [3, 8], replicated, may hold values from 0.3 to 1
Outputs:
- coulomb_change: float32 [8, 1024, 1024], P('depth', 'wave')
Inputs may be any that keep to these rules, and one draw needn't show every extreme that they name: `slice_layer`: never falls along the column; 0 at the first slice and 15 at the last.
All inputs are finite; a program needn't handle non-finite values. No bound on the sum of `slip_mask` on one device may be relied on, other than what follows from the above.
Results may differ from a plain program's by a relative error of at most 0.0015.
Values may be sent and summed in bfloat16 or wider, within the bound.
A program may use at most 64 MiB of HBM per device.

v0:
```python
import math

import jax
import jax.numpy as jnp
from jax import lax
from jax.sharding import PartitionSpec as P

S = 16
R = 8


radix_first = 32
slice_thick = 0.1
highest = lax.Precision.HIGHEST


def phase_table(row_count, col_count, period, direction):
    product = lax.broadcasted_iota(jnp.int32, (row_count, col_count), 0) * lax.broadcasted_iota(
        jnp.int32, (row_count, col_count), 1
    )
    phase_angle = (product % period).astype(jnp.float32) * (direction * 2.0 * math.pi / period)
    return (jnp.cos(phase_angle), jnp.sin(phase_angle))


def complex_einsum(einsum_form, real_part, imag_part, twiddle):
    cosine, sine_part = twiddle
    first = jnp.einsum(einsum_form, real_part, cosine, precision=highest)
    second = jnp.einsum(einsum_form, real_part, sine_part, precision=highest)
    if imag_part is None:
        return (first, second)
    return (
        first - jnp.einsum(einsum_form, imag_part, sine_part, precision=highest),
        second + jnp.einsum(einsum_form, imag_part, cosine, precision=highest),
    )


def rotate(real_part, imag_part, twiddle):
    cosine, sine_part = twiddle
    return (real_part * cosine - imag_part * sine_part, real_part * sine_part + imag_part * cosine)


def transform_last(real_part, imag_part, direction):
    length = real_part.shape[-1]
    second_len = length // radix_first
    leading = real_part.shape[:-1]
    split_shape = leading + (radix_first, second_len)
    shaped_imag = None if imag_part is None else imag_part.reshape(split_shape)
    section_real, section_imag = complex_einsum(
        "...pq,pa->...aq",
        real_part.reshape(split_shape),
        shaped_imag,
        phase_table(radix_first, radix_first, radix_first, direction),
    )
    section_real, section_imag = rotate(
        section_real, section_imag, phase_table(radix_first, second_len, length, direction)
    )
    final_real, final_imag = complex_einsum(
        "...aq,qb->...ba",
        section_real,
        section_imag,
        phase_table(second_len, second_len, second_len, direction),
    )
    norm_scale = 1.0 / math.sqrt(length)
    return (
        final_real.reshape(leading + (length,)) * norm_scale,
        final_imag.reshape(leading + (length,)) * norm_scale,
    )


def transform_cols(real_part, imag_part, direction, real_only):
    length = real_part.shape[-2]
    columns = real_part.shape[-1]
    second_len = length // radix_first
    leading = real_part.shape[:-2]
    split_shape = leading + (radix_first, second_len, columns)
    section_real, section_imag = complex_einsum(
        "...ngs,nl->...lgs",
        real_part.reshape(split_shape),
        imag_part.reshape(split_shape),
        phase_table(radix_first, radix_first, radix_first, direction),
    )
    cosine, sine_part = phase_table(radix_first, second_len, length, direction)
    section_real, section_imag = rotate(
        section_real, section_imag, (cosine[:, :, None], sine_part[:, :, None])
    )
    last_cos, last_sin = phase_table(second_len, second_len, second_len, direction)
    norm_scale = 1.0 / math.sqrt(length)
    if real_only:
        final_real = jnp.einsum(
            "...aqm,qb->...mba", section_real, last_cos, precision=highest
        ) - jnp.einsum("...aqm,qb->...mba", section_imag, last_sin, precision=highest)
        return final_real.reshape(leading + (columns, length)) * norm_scale
    final_real, final_imag = complex_einsum(
        "...aqm,qb->...mba", section_real, section_imag, (last_cos, last_sin)
    )
    return (
        final_real.reshape(leading + (columns, length)) * norm_scale,
        final_imag.reshape(leading + (columns, length)) * norm_scale,
    )


def signed_index(ladder, length):
    return ((ladder + length // 2) % length - length // 2).astype(jnp.float32)


def wave_geometry(row_ladder, col_ladder, length):
    y_wave = signed_index(row_ladder, length)[:, None]
    x_wave = signed_index(col_ladder, length)[None, :]
    magnitude = jnp.sqrt(x_wave * x_wave + y_wave * y_wave)
    bounded = jnp.maximum(magnitude, 1.0)
    return (2.0 * math.pi / length * magnitude, x_wave / bounded, y_wave / bounded)


def depth_column(slice_layer, layer_material, materials):
    layer_count = layer_material.shape[0]
    kind_count = materials.shape[1]
    matches = slice_layer[:, None] == jnp.arange(layer_count, dtype=jnp.int32)[None, :]
    chosen = jnp.sum(jnp.where(matches, layer_material[None, :], 0), axis=1)
    one_hot = (chosen[:, None] == jnp.arange(kind_count, dtype=jnp.int32)[None, :]).astype(
        jnp.float32
    )
    properties = jnp.dot(one_hot, materials.T, precision=highest)
    thickness = slice_thick * properties[:, 0]
    center = jnp.cumsum(thickness) - 0.5 * thickness
    return (center, properties[:, 1], properties[:, 2])


def contract(spec_real, spec_imag, source_depth, receiver_depth, geometry, totals):
    wave_num, along_x, along_y = geometry
    receiver_col = receiver_depth[:, None, None]

    def add_source(source_index, running):
        acc_real, acc_imag = running
        first_real = spec_real[source_index, 0].astype(jnp.float32)
        second_real = spec_real[source_index, 1].astype(jnp.float32)
        first_imag = spec_imag[source_index, 0].astype(jnp.float32)
        second_imag = spec_imag[source_index, 1].astype(jnp.float32)
        near_gap = jnp.abs(receiver_col - source_depth[source_index])
        far_sum = receiver_col + source_depth[source_index]
        direct = jnp.exp(-wave_num * near_gap)
        mirror = jnp.exp(-wave_num * far_sum)
        summed = direct + mirror
        slope_term = wave_num * (near_gap * direct - far_sum * mirror)
        strike = summed - along_x * along_x * slope_term
        cross_term = -along_x * along_y * slope_term
        dipping = summed - along_y * along_y * slope_term
        normal_part = summed - slope_term
        add_real = jnp.stack(
            [
                strike * first_real + cross_term * second_real,
                cross_term * first_real + dipping * second_real,
                -normal_part * (along_x * first_imag + along_y * second_imag),
            ],
            axis=1,
        )
        add_imag = jnp.stack(
            [
                strike * first_imag + cross_term * second_imag,
                cross_term * first_imag + dipping * second_imag,
                normal_part * (along_x * first_real + along_y * second_real),
            ],
            axis=1,
        )
        return (acc_real + add_real, acc_imag + add_imag)

    return lax.fori_loop(0, spec_real.shape[0], add_source, totals)


def finish_forward(pieces):
    out_real, out_imag = transform_cols(pieces[0], pieces[1], -1.0, False)
    return (out_real.astype(jnp.bfloat16), out_imag.astype(jnp.bfloat16))


def shards(slip_field, slip_mask, slice_layer, layer_material, materials):
    local_sources = slip_field.shape[0]
    grid_len = slip_field.shape[3]
    tile_rows = slip_field.shape[2] // slip_mask.shape[1]
    tile_cols = grid_len // slip_mask.shape[2]
    shaped = slip_field.reshape(
        (local_sources, 2, slip_mask.shape[1], tile_rows, slip_mask.shape[2], tile_cols)
    )
    masked = shaped.astype(jnp.float32) * slip_mask.astype(jnp.float32)[:, None, :, None, :, None]
    slip_cells = masked.reshape(slip_field.shape)
    half_real, half_imag = transform_last(slip_cells, None, -1.0)
    center, rigidity, friction = depth_column(slice_layer, layer_material, materials)
    depth_count = slice_layer.shape[0]
    source_depth = center.reshape((S, depth_count // S))[:, depth_count // (4 * S)]
    receiver_offset = depth_count // (2 * R) - 1
    receiver_depth = center.reshape((R, depth_count // R))[:, receiver_offset]
    receiver_rigid = rigidity.reshape((R, depth_count // R))[:, receiver_offset]
    receiver_fric = friction.reshape((R, depth_count // R))[:, receiver_offset]
    per_device = R // lax.axis_size("depth")
    first_receiver = lax.axis_index("depth") * per_device
    local_depth = lax.dynamic_slice_in_dim(receiver_depth, first_receiver, per_device)
    local_rigid = lax.dynamic_slice_in_dim(receiver_rigid, first_receiver, per_device)
    local_fric = lax.dynamic_slice_in_dim(receiver_fric, first_receiver, per_device)
    spec_real, spec_imag = finish_forward(
        (
            lax.all_to_all(half_real, "wave", split_axis=3, concat_axis=2, tiled=True),
            lax.all_to_all(half_imag, "wave", split_axis=3, concat_axis=2, tiled=True),
        )
    )
    rows_here = spec_real.shape[2]
    row_ladder = lax.axis_index("wave") * rows_here + jnp.arange(rows_here, dtype=jnp.int32)
    geometry = wave_geometry(row_ladder, jnp.arange(grid_len, dtype=jnp.int32), grid_len)
    empty_sum = jnp.zeros((per_device, 3, rows_here, grid_len), jnp.float32)
    trac_real, trac_imag = contract(
        lax.all_gather(spec_real, "depth", axis=0, tiled=True),
        lax.all_gather(spec_imag, "depth", axis=0, tiled=True),
        source_depth,
        local_depth,
        geometry,
        (empty_sum, empty_sum),
    )
    weights = jnp.stack([local_rigid, local_rigid, local_rigid * local_fric], axis=1)[
        :, :, None, None
    ]
    inv_real, inv_imag = transform_last(trac_real * weights, trac_imag * weights, 1.0)
    stress = transform_cols(
        lax.all_to_all(inv_real, "wave", split_axis=3, concat_axis=2, tiled=True),
        lax.all_to_all(inv_imag, "wave", split_axis=3, concat_axis=2, tiled=True),
        1.0,
        True,
    )
    return jnp.sqrt(stress[:, 0] * stress[:, 0] + stress[:, 1] * stress[:, 1] + 1.0) + stress[:, 2]


def solution(mesh):
    placed = (P("depth", None, "wave", None), P("depth", "wave", None), P(), P(), P())
    return jax.shard_map(
        shards, mesh=mesh, in_specs=placed, out_specs=P("depth", "wave", None), check_vma=False
    )
```

profile of v0, /device:TPU:1, one launch (start us, length us, event | category | flops | bytes accessed | tf_op | source)
XLA Modules:
  0.0 475.9 jit_solution(12923932934051112682)
XLA Ops:
  6.5 2.9 reshape.912
  9.4 3.7 fusion.63
  13.1 3.3 fusion.65
  16.6 11.4 %fusion.47 = f32[32,2,2,32,32]{4,0,3,2,1:T(8,128)S(1)} fusion(f32[32,2,2,32,32]{4,0,3,2,1:T(8,128)S(1)} %fusion.63, f32[32,2,2,32,32]{4,0,3,2,1:T(8,128)} %fusion.65, f32[32,32]{1,0:T(8,128)S(1)} %copy.82, f32[32,32]{1,0:T(8,128)S(1)} %copy.81), kind=kOutput, calls=%fused_computation.61 | convolution fusion | flops 50739200 | bytes 1581056 | tf_op jit(solution)/shard_map/...aq,qb->...ba/dot_general | solution.py:33
  28.1 21.7 %multiply_bitcast_fusion = f32[2,2,32,32,32]{4,3,2,1,0:T(8,128)} fusion(f32[32,2,2,32,32]{4,0,3,2,1:T(8,128)S(1)} %fusion.47, f32[32,2,2,32,32]{4,0,3,2,1:T(8,128)S(1)} %fusion.63, f32[32,2,2,32,32]{4,0,3,2,1:T(8,128)S(1)} %copy-done.2, f32[32,32]{1,0:T(8,128)S(1)} %copy.82, f32[32,32]{1,0:T(8,128)S(1)} %copy.81), kind=kOutput, calls=%fused_computation.73 | convolution fusion | flops 51001344 | bytes 2105344 | tf_op jit(solution)/shard_map/...aq,qb->...ba/dot_general | solution.py:28
  49.7 4.1 copy.108
  53.8 4.3 reshape.948
  58.1 11.0 %all-to-all-start.1 = ((f32[32,1,4096]{2,1,0:T(1,128)}), f32[32,1,4096]{2,1,0:T(1,128)S(1)}, u32[]{:S(2)}, u32[]{:S(2)}) async-start(f32[32,1,4096]{2,1,0:T(1,128)} %reshape.948), calls=%async_computation.1 | async-start | bytes 1048576 | tf_op jit(solution)/shard_map/all_to_all | solution.py:200
  69.2 11.4 %fusion.49 = f32[32,2,2,32,32]{4,0,3,2,1:T(8,128)S(1)} fusion(f32[32,2,2,32,32]{4,0,3,2,1:T(8,128)S(1)} %fusion.63, f32[32,2,2,32,32]{4,0,3,2,1:T(8,128)} %fusion.65, f32[32,32]{1,0:T(8,128)S(1)} %copy.82, f32[32,32]{1,0:T(8,128)S(1)} %copy.81), kind=kOutput, calls=%fused_computation.63 | convolution fusion | flops 50739200 | bytes 1581056 | tf_op jit(solution)/shard_map/...aq,qb->...ba/dot_general | solution.py:32
  80.6 11.0 %multiply_bitcast_fusion.1 = f32[2,2,32,32,32]{4,3,2,1,0:T(8,128)} fusion(f32[32,2,2,32,32]{4,0,3,2,1:T(8,128)S(1)} %fusion.49, f32[32,2,2,32,32]{4,0,3,2,1:T(8,128)S(1)} %fusion.63, f32[32,2,2,32,32]{4,0,3,2,1:T(8,128)S(1)} %copy-done.3, f32[32,32]{1,0:T(8,128)S(1)} %copy.82, f32[32,32]{1,0:T(8,128)S(1)} %copy.81), kind=kOutput, calls=%fused_computation.74 | convolution fusion | flops 51001344 | bytes 2105344 | tf_op jit(solution)/shard_map/...aq,qb->...ba/dot_general | solution.py:27
  91.6 3.1 copy.106
  94.7 2.9 reshape.950
  97.6 8.3 %all-to-all-start = ((f32[32,1,4096]{2,1,0:T(1,128)}), f32[32,1,4096]{2,1,0:T(1,128)S(1)}, u32[]{:S(2)}, u32[]{:S(2)}) async-start(f32[32,1,4096]{2,1,0:T(1,128)} %reshape.950), calls=%async_computation | async-start | bytes 1048576 | tf_op jit(solution)/shard_map/all_to_all | solution.py:199
  106.8 1.9 reduce.16
  108.7 3.1 reshape.949
  111.8 3.0 copy.109
  114.9 3.3 fusion.41
  118.1 3.3 fusion.39
  122.4 1.9 reduce.17
  124.3 3.1 reshape.951
  127.4 3.2 copy.107
  130.6 3.8 fusion.71
  134.4 2.7 subtract_bitcast_fusion
  137.1 3.0 fusion.55
  140.2 3.1 fusion.122
  143.2 2.4 copy.92
  145.6 1.9 convert_element_type.283
  147.6 4.7 fusion.57
  152.3 3.1 fusion.119
  155.4 2.2 copy.89
  157.6 1.9 convert_element_type.280
  166.1 39.2 %all-gather.5.cloned.1.call-done = bf16[16,2,32,1024]{3,2,1,0:T(8,128)(2,1)} async-done(((bf16[2,2,32,1024]{3,2,1,0:T(8,128)(2,1)}), bf16[16,2,32,1024]{3,2,1,0:T(8,128)(2,1)}) %all-gather.5.cloned.1.call-update) | async-done | bytes 2097168 | tf_op jit(solution)/shard_map/all_gather | solution.py:209
  205.3 59.2 %all-gather.3.cloned.1.call-done = bf16[16,2,32,1024]{3,2,1,0:T(8,128)(2,1)} async-done(((bf16[2,2,32,1024]{3,2,1,0:T(8,128)(2,1)}), bf16[16,2,32,1024]{3,2,1,0:T(8,128)(2,1)}) %all-gather.3.cloned.1.call-update) | async-done | bytes 2097168 | tf_op jit(solution)/shard_map/all_gather | solution.py:208
  264.4 78.1 %while.21 = (s32[]{:T(128)}, f32[1,3,32,1024]{3,2,1,0:T(8,128)S(1)}, f32[1,3,32,1024]{3,2,1,0:T(8,128)S(1)}, f32[16]{0:T(128)S(1)}, f32[1,1,1]{2,1,0:T(1,128)}, ...) while((s32[]{:T(128)}, ...), condition=%wide.region_3.4_spmd.clone.clone.clone, body=%wide.region_2.3_spmd.clone.clone.clone.sunk | while | flops 2523142 | bytes 3426495 | solution.py:166
  343.2 2.7 fusion.166
  345.9 2.7 fusion.143
  350.3 3.0 convolution_subtract_fusion
  353.4 2.9 convolution_add_fusion
  356.3 7.2 %fusion.89 = f32[32,3,32,32]{3,0,2,1:T(8,128)S(1)} fusion(f32[32,3,32,32]{3,0,2,1:T(8,128)S(1)} %convolution_add_fusion, f32[32,3,32,32]{3,0,2,1:T(8,128)S(1)} %convolution_subtract_fusion, f32[32,32]{1,0:T(8,128)S(1)} %copy-done.14, f32[32,32]{1,0:T(8,128)S(1)} %copy-done.12), kind=kOutput, calls=%fused_computation.107 | convolution fusion | flops 38057984 | bytes 1187840 | tf_op jit(solution)/shard_map/...aq,qb->...ba/dot_general | solution.py:33
  363.6 8.6 %multiply_bitcast_fusion.3 = f32[1,3,32,32,32]{4,3,2,1,0:T(8,128)} fusion(f32[32,3,32,32]{3,0,2,1:T(8,128)S(1)} %fusion.89, f32[32,3,32,32]{3,0,2,1:T(8,128)S(1)} %convolution_add_fusion, f32[32,3,32,32]{3,0,2,1:T(8,128)S(1)} %convolution_subtract_fusion, f32[32,32]{1,0:T(8,128)S(1)} %copy-done.14, f32[32,32]{1,0:T(8,128)S(1)} %copy-done.12), kind=kOutput, calls=%fused_computation.126 | convolution fusion | flops 38254592 | bytes 1581056 | tf_op jit(solution)/shard_map/...aq,qb->...ba/dot_general | solution.py:28
  372.1 2.1 mul.1439
  374.2 2.8 copy.97
  377.0 7.7 %reduce.18 = f32[1024,3,32]{2,1,0:T(4,128)} reduce(f32[1024,3,1,32]{3,2,1,0:T(1,128)} %bitcast.324, f32[]{:T(128)} %broadcast.1179), dimensions={2}, to_apply=%bitcast.295.reduce_sub_computation | reduce | bytes 786436
  384.8 3.6 reshape.952
  388.3 8.9 %all-to-all-start.3 = ((f32[32,1,3072]{2,1,0:T(1,128)}), f32[32,1,3072]{2,1,0:T(1,128)S(1)}, u32[]{:S(2)}, u32[]{:S(2)}) async-start(f32[32,1,3072]{2,1,0:T(1,128)} %reshape.952), calls=%async_computation.3 | async-start | bytes 786432 | tf_op jit(solution)/shard_map/all_to_all | solution.py:221
  397.2 8.0 %fusion.91 = f32[32,3,32,32]{3,0,2,1:T(8,128)S(1)} fusion(f32[32,3,32,32]{3,0,2,1:T(8,128)S(1)} %convolution_add_fusion, f32[32,3,32,32]{3,0,2,1:T(8,128)S(1)} %convolution_subtract_fusion, f32[32,32]{1,0:T(8,128)} %copy.94, f32[32,32]{1,0:T(8,128)} %copy.93), kind=kOutput, calls=%fused_computation.109 | convolution fusion | flops 38057984 | bytes 1187840 | tf_op jit(solution)/shard_map/...aq,qb->...ba/dot_general | solution.py:32
  405.3 8.4 %multiply_bitcast_fusion.4 = f32[1,3,32,32,32]{4,3,2,1,0:T(8,128)} fusion(f32[32,3,32,32]{3,0,2,1:T(8,128)S(1)} %fusion.91, f32[32,3,32,32]{3,0,2,1:T(8,128)S(1)} %convolution_add_fusion, f32[32,3,32,32]{3,0,2,1:T(8,128)S(1)} %convolution_subtract_fusion, f32[32,32]{1,0:T(8,128)S(1)} %copy-done.15, f32[32,32]{1,0:T(8,128)S(1)} %copy-done.13), kind=kOutput, calls=%fused_computation.127 | convolution fusion | flops 38254592 | bytes 1581056 | tf_op jit(solution)/shard_map/...aq,qb->...ba/dot_general | solution.py:27
  413.7 2.1 mul.1435
  415.9 2.8 copy.95
  418.7 6.4 %reduce.20 = f32[1024,3,32]{2,1,0:T(4,128)S(1)} reduce(f32[1024,3,1,32]{3,2,1,0:T(1,128)} %bitcast.325, f32[]{:T(128)} %broadcast.1179), dimensions={2}, to_apply=%bitcast.297.reduce_sub_computation | reduce | bytes 786436
  425.1 2.4 reshape.954
  427.5 8.3 %all-to-all-start.2 = ((f32[32,1,3072]{2,1,0:T(1,128)}), f32[32,1,3072]{2,1,0:T(1,128)}, u32[]{:S(2)}, u32[]{:S(2)}) async-start(f32[32,1,3072]{2,1,0:T(1,128)} %reshape.954), calls=%async_computation.2 | async-start | bytes 786432 | tf_op jit(solution)/shard_map/all_to_all | solution.py:220
  437.3 2.7 reshape.953
  440.0 1.8 copy.98
  443.8 2.7 fusion.81
  446.5 3.1 all-to-all-done.2
  449.6 2.5 reduce.21
  452.1 2.7 reshape.955
  454.8 1.9 copy.96
  457.3 1.6 fusion.113
  459.0 2.1 fusion.78
  461.1 2.3 fusion.99
  463.4 2.4 multiply_bitcast_fusion.2
  465.8 1.6 copy.101
  (143 shorter events, 51.9 us)
Async XLA Ops:
  6.5 153.1 %copy-start = (f32[3,8]{1,0:T(4,128)S(1)}, f32[3,8]{1,0:T(4,128)}, u32[]{:S(2)}) copy-start(f32[3,8]{1,0:T(4,128)} %param.11) | copy-start | bytes 292
  6.5 2.9 copy-start.20
  9.4 3.7 copy-start.7
  16.6 11.4 %copy-start.2 = (f32[32,2,2,32,32]{4,0,3,2,1:T(8,128)S(1)}, f32[32,2,2,32,32]{4,0,3,2,1:T(8,128)}, u32[]{:S(2)}) copy-start(f32[32,2,2,32,32]{4,0,3,2,1:T(8,128)} %fusion.65) | copy-start | bytes 1572868
  58.1 39.5 %all-to-all-start.1 = ((f32[32,1,4096]{2,1,0:T(1,128)}), f32[32,1,4096]{2,1,0:T(1,128)S(1)}, u32[]{:S(2)}, u32[]{:S(2)}) async-start(f32[32,1,4096]{2,1,0:T(1,128)} %reshape.948), calls=%async_computation.1 | async-start | bytes 1048576 | tf_op jit(solution)/shard_map/all_to_all | solution.py:200
  69.2 11.4 %copy-start.3 = (f32[32,2,2,32,32]{4,0,3,2,1:T(8,128)S(1)}, f32[32,2,2,32,32]{4,0,3,2,1:T(8,128)}, u32[]{:S(2)}) copy-start(f32[32,2,2,32,32]{4,0,3,2,1:T(8,128)} %fusion.65) | copy-start | bytes 1572868
  97.6 24.8 %all-to-all-start = ((f32[32,1,4096]{2,1,0:T(1,128)}), f32[32,1,4096]{2,1,0:T(1,128)S(1)}, u32[]{:S(2)}, u32[]{:S(2)}) async-start(f32[32,1,4096]{2,1,0:T(1,128)} %reshape.950), calls=%async_computation | async-start | bytes 1048576 | tf_op jit(solution)/shard_map/all_to_all | solution.py:199
  105.9 99.4 %all-gather.5.cloned.1.call-start = ((), (), s32[]{:S(2)}) async-start(), calls=%async_computation.5 | async-start | bytes 2359296 | tf_op jit(solution)/shard_map/all_gather | solution.py:209
  130.6 3.8 copy-start.9
  137.1 3.0 copy-start.6
  137.1 3.0 copy-start.4
  147.5 4.8 %copy-start.5 = (f32[2,2,32,32,32]{4,2,3,1,0:T(8,128)S(1)}, f32[2,2,32,32,32]{4,2,3,1,0:T(8,128)}, u32[]{:S(2)}) copy-start(f32[2,2,32,32,32]{4,2,3,1,0:T(8,128)} %copy-done.4) | copy-start | bytes 1572868
  147.5 116.9 %all-gather.3.cloned.1.call-start = ((), (), s32[]{:S(2)}) async-start(), calls=%async_computation.4 | async-start | bytes 2359296 | tf_op jit(solution)/shard_map/all_gather | solution.py:208
  155.4 4.1 copy-start.21
  155.4 4.1 copy-start.22
  161.9 102.5 %copy-start.16 = (f32[32,32]{0,1:T(8,128)}, f32[32,32]{0,1:T(8,128)S(1)}, u32[]{:S(2)}) copy-start(f32[32,32]{0,1:T(8,128)S(1)} %get-tuple-element.539) | copy-start | bytes 12292
  162.0 102.5 %copy-start.18 = (f32[32,32]{0,1:T(8,128)}, f32[32,32]{0,1:T(8,128)S(1)}, u32[]{:S(2)}) copy-start(f32[32,32]{0,1:T(8,128)S(1)} %get-tuple-element.540) | copy-start | bytes 12292
  349.1 1.2 copy-start.8
  350.3 3.1 copy-start.10
  353.3 3.0 copy-start.12
  353.3 3.0 copy-start.14
  388.3 39.1 %all-to-all-start.3 = ((f32[32,1,3072]{2,1,0:T(1,128)}), f32[32,1,3072]{2,1,0:T(1,128)S(1)}, u32[]{:S(2)}, u32[]{:S(2)}) async-start(f32[32,1,3072]{2,1,0:T(1,128)} %reshape.952), calls=%async_computation.3 | async-start | bytes 786432 | tf_op jit(solution)/shard_map/all_to_all | solution.py:221
  397.2 8.1 %copy-start.13 = (f32[32,32]{1,0:T(8,128)S(1)}, f32[32,32]{1,0:T(8,128)}, u32[]{:S(2)}) copy-start(f32[32,32]{1,0:T(8,128)} %copy.93) | copy-start | bytes 12292
  397.2 8.1 %copy-start.15 = (f32[32,32]{1,0:T(8,128)S(1)}, f32[32,32]{1,0:T(8,128)}, u32[]{:S(2)}) copy-start(f32[32,32]{1,0:T(8,128)} %copy.94) | copy-start | bytes 12292
  427.5 22.1 %all-to-all-start.2 = ((f32[32,1,3072]{2,1,0:T(1,128)}), f32[32,1,3072]{2,1,0:T(1,128)}, u32[]{:S(2)}, u32[]{:S(2)}) async-start(f32[32,1,3072]{2,1,0:T(1,128)} %reshape.954), calls=%async_computation.2 | async-start | bytes 786432 | tf_op jit(solution)/shard_map/all_to_all | solution.py:220
  457.3 1.7 copy-start.11
  457.3 1.7 copy-start.17
  457.3 1.7 copy-start.19
  463.4 5.5 %copy-start.1 = (f32[3,8]{1,0:T(4,128)S(1)}, f32[3,8]{1,0:T(4,128)}, u32[]{:S(2)}) copy-start(f32[3,8]{1,0:T(4,128)} %param.11) | copy-start | bytes 292
Sparse Core Ops, SparseCore 0:
  147.6 57.6 all-gather.4
  207.9 56.4 all-gather.2
where the time goes:
time: 482 us; the launch traced here: 476 us
  matrix products  146 us (30%)
  waiting for transfers between devices  102 us (21%)
  local copies, waits for them, and re-layouts  83.1 us (17%)
  other arithmetic  50.4 us (10%)
  loops' own time  43 us (9%)
  starting transfers between devices  37 us (8%)
  between operations  14.2 us (3%)
    all_gather x1, waiting for transfers between devices, shards(): lax.all_gather(spec_real, 'depth', axis=0, tiled=True)  59.2 us
    dot_general x7, matrix products, complex_einsum(): second = jnp.einsum(einsum_form, real_part, sine_part, precision=highest)  44.4 us
    another operation x1, loops' own time, contract(): return lax.fori_loop(0, spec_real.shape[0], add_source, totals)  43 us
    all_gather x1, waiting for transfers between devices, shards(): lax.all_gather(spec_imag, 'depth', axis=0, tiled=True)  39.2 us
    dot_general x7, matrix products, complex_einsum(): first = jnp.einsum(einsum_form, real_part, cosine, precision=highest)  33.8 us
    dot_general x6, matrix products, complex_einsum(): jnp.einsum(einsum_form, imag_part, sine_part, precision=highest)  32 us
    dot_general x6, matrix products, complex_einsum(): jnp.einsum(einsum_form, imag_part, cosine, precision=highest)  30.6 us
    unnamed x54, local copies, waits for them, and re-layouts  26 us
  transfers between devices with their start and end apart: 6, of which 4 were waited for; matrix products, arithmetic and copies ran while one was open for 21% of the time, Pallas kernels for 0%

commit v1 on v0

v1 whole, which is shorter than its diff:
```python
import functools
import math

import jax
import jax.numpy as jnp
import ml_dtypes
import numpy as np
from jax import lax
from jax.experimental import pallas as pl
from jax.experimental.pallas import tpu as pltpu
from jax.sharding import PartitionSpec as P

GRID = 1024
HALF = 512
QUARTER = 256
S = 16
R = 8
NZ = 64
DEVICES = 256
BF16 = jnp.bfloat16
F32 = jnp.float32
VMEM = pltpu.VMEM
SMEM = pltpu.SMEM


def split_table(table):
    high = table.astype(ml_dtypes.bfloat16)
    low = (table - high.astype(np.float64)).astype(ml_dtypes.bfloat16)
    return np.stack([high, low])


def tables():
    j = np.arange(QUARTER, dtype=np.int64)[:, None]
    cell = np.arange(HALF, dtype=np.int64)[None, :]
    rows = []
    for parity in range(2):
        angle = 2.0 * np.pi * (((2 * j + parity) * cell) % GRID) / GRID
        real, imag = np.cos(angle), -np.sin(angle)
        if parity == 0:
            imag[0] = 1.0 - 2.0 * (cell[0] % 2)
        rows += [real, imag]
    real_dft = np.concatenate(rows) / 32.0
    k = np.arange(QUARTER, dtype=np.int64)
    angle = 2.0 * np.pi * ((k[:, None] * k[None, :]) % QUARTER) / QUARTER
    cosine, sine = np.cos(angle) / 32.0, np.sin(angle) / 32.0
    complex_dft = np.block([[cosine, -sine], [sine, cosine]])
    turn = 2.0 * np.pi * np.arange(4)[:, None] * k[None, :] / GRID
    twiddle = np.concatenate([np.cos(turn), -np.sin(turn)]).astype(np.float32)
    return split_table(real_dft), split_table(complex_dft), twiddle


def halves(value):
    high = value.astype(BF16)
    return high, (value - high.astype(F32)).astype(BF16)


def dot(left, right, transposed=False):
    dims = (((1,), (1 if transposed else 0,)), ((), ()))
    return lax.dot_general(left, right, dims, preferred_element_type=F32)


def forward_rows(mask_ref, slip_ref, table_ref, out_ref):
    tile = lax.broadcasted_iota(jnp.int32, (32, GRID), 0)
    cell = lax.broadcasted_iota(jnp.int32, (32, GRID), 1)
    spread = (cell // 32 == tile).astype(BF16)
    mask = dot(mask_ref[...].astype(F32).astype(BF16), spread)
    slip = slip_ref[...].astype(F32)
    rows = slip.shape[0] // 2
    cells = jnp.concatenate([slip[:rows] * mask[0:1], slip[rows:] * mask[1:2]], axis=0)
    near, far = cells[:, :HALF], cells[:, HALF:]
    for parity, combined in enumerate((near + far, near - far)):
        high, low = halves(combined)
        part = slice(parity * HALF, (parity + 1) * HALF)
        result = (
            dot(table_ref[0, part], high, True)
            + dot(table_ref[0, part], low, True)
            + dot(table_ref[1, part], high, True)
        )
        for imag in range(2):
            out_ref[pl.ds(2 * parity + imag, QUARTER, stride=4), :] = result[
                imag * QUARTER : (imag + 1) * QUARTER
            ]


def swap_groups(items):
    lane = lax.broadcasted_iota(jnp.int32, items[0].shape, 1)
    for width in (2, 1):
        size = 32 * width
        upper = (lane // size) % 2 == 1
        out = list(items)
        for a in range(4):
            if a & width:
                continue
            b = a | width
            first, second = items[a], items[b]
            out[a] = jnp.where(upper, pltpu.roll(second, size, 1), first)
            out[b] = jnp.where(upper, second, pltpu.roll(first, 128 - size, 1))
        items = out
    return items


def radix_four(items):
    (r0, i0), (r1, i1), (r2, i2), (r3, i3) = items
    ar, ai, br, bi = r0 + r2, i0 + i2, r0 - r2, i0 - i2
    cr, ci, dr, di = r1 + r3, i1 + i3, r1 - r3, i1 - i3
    return [
        (ar + cr, ai + ci),
        (br + di, bi - dr),
        (ar - cr, ai - ci),
        (br - di, bi + dr),
    ]


def times(item, cosine, sine):
    real, imag = item
    return real * cosine - imag * sine, real * sine + imag * cosine


def depths(slice_ref, layer_ref, material_ref):
    center, rigidity, friction = [], [], []
    top = None
    for place in range(NZ):
        kind = layer_ref[slice_ref[place]]
        thickness = jnp.float32(0.1) * material_ref[kind]
        top = thickness if top is None else top + thickness
        center.append(top - 0.5 * thickness)
        if place % 8 == 3:
            rigidity.append(material_ref[8 + kind])
            friction.append(material_ref[16 + kind])
    source = [center[4 * s + 1] for s in range(S)]
    receiver = [center[8 * r + 3] for r in range(R)]
    return source, receiver, rigidity, friction


def geometry(first_row, rows, half, ky):
    k0 = lax.broadcasted_iota(jnp.int32, (rows, 128), 0) % 4
    k1 = lax.broadcasted_iota(jnp.int32, (rows, 128), 1) + 128 * half
    kx = 4 * k1 + k0
    signed = jnp.where(kx >= HALF, kx - GRID, kx)
    x_wave, y_wave = signed.astype(F32), ky.astype(F32)
    magnitude = jnp.sqrt(x_wave * x_wave + y_wave * y_wave)
    bounded = jnp.maximum(magnitude, 1.0)
    along_x, along_y = x_wave / bounded, y_wave / bounded
    x_edge, y_edge = signed == -HALF, ky == -HALF
    cross = jnp.where(x_edge != y_edge, 0.0, along_x * along_y)
    odd_x = jnp.where(x_edge, 0.0, along_x)
    odd_y = jnp.where(y_edge, 0.0, along_y)
    wave = 2.0 * math.pi / GRID * magnitude
    return wave, along_x * along_x, cross, along_y * along_y, odd_x, odd_y


def middle(
    position,
    slice_ref,
    layer_ref,
    material_ref,
    table_ref,
    twiddle_ref,
    got_ref,
    out_ref,
    left_ref,
    spec_ref,
    edge_ref,
    suffix_ref,
    trac_ref,
):
    j = position()
    first = j == 0
    source, receiver, rigidity, friction = depths(slice_ref, layer_ref, material_ref)
    keep_imag = jnp.where(first, 0.0, 1.0).astype(F32)
    only_first = 1.0 - keep_imag
    cosines = [twiddle_ref[a : a + 1, :] for a in range(4)]
    sines = [twiddle_ref[4 + a : 5 + a, :] for a in range(4)]

    loaded = [got_ref[pl.ds(c, DEVICES, stride=4), :] for c in range(4)]
    blocks = [[[None] * 8 for _ in range(4)] for _ in range(4)]
    for c in range(4):
        for outer in range(8):
            group = swap_groups([loaded[c][(4 * outer + inner) * 8 : (4 * outer + inner) * 8 + 8] for inner in range(4)])
            for g in range(4):
                blocks[c][g][outer] = group[g]
    for g in range(4):
        whole = [
            [jnp.concatenate([blocks[c][g][2 * x0], blocks[c][g][2 * x0 + 1]], axis=1) for x0 in range(4)]
            for c in range(4)
        ]
        kinds = [
            [(whole[0][x0], whole[1][x0] * keep_imag) for x0 in range(4)],
            [(whole[2][x0], whole[3][x0]) for x0 in range(4)],
            [(whole[1][x0], jnp.zeros_like(whole[1][x0])) for x0 in range(4)],
        ]
        for p in range(3):
            mixed = radix_four(kinds[p])
            for k0 in range(4):
                real, imag = times(mixed[k0], cosines[k0], sines[k0])
                if p < 2:
                    place = pl.ds(64 * g + 4 * p + k0, 8, stride=8)
                else:
                    place = pl.ds(256 + 32 * g + k0, 8, stride=4)
                for t in range(2):
                    left_ref.at[t][place, :] = real[:, 128 * t : 128 * t + 128]
                    left_ref.at[2 + t][place, :] = imag[:, 128 * t : 128 * t + 128]
    high, low = halves(jnp.concatenate([left_ref[t] for t in range(4)], axis=1))
    spectra = dot(high, table_ref[0]) + dot(low, table_ref[0]) + dot(high, table_ref[1])
    spec_ref[...] = spectra.astype(BF16).astype(F32)

    def unit(rows, base, step, half, ky, row_weight, write):
        wave, uu, uv, vv, odd_x, odd_y = geometry(0, rows, half, ky)

        def fields(s):
            picked = []
            for q in range(2):
                row = base + (2 * (s % 2) + q) * 8 * step + (s // 2) * step
                for imag in range(2):
                    start = 256 * imag + 128 * half
                    picked.append(spec_ref[row : row + rows, start : start + 128])
            return picked

        zero = jnp.zeros((rows, 128), F32)
        suffix, moment = [zero] * 4, [zero] * 4
        for s in reversed(range(S)):
            decay = jnp.exp(-wave * source[s])
            values = fields(s)
            scaled = [decay * value for value in values]
            suffix = [a + b for a, b in zip(suffix, scaled)]
            moment = [a + source[s] * b for a, b in zip(moment, scaled)]
            if s % 2 == 1:
                for n in range(4):
                    suffix_ref[s // 2, n, 0:rows, :] = suffix[n]
                    suffix_ref[s // 2, 4 + n, 0:rows, :] = moment[n]
        total, total_moment = suffix, moment
        prefix, moment = [zero] * 4, [zero] * 4
        for s in range(S - 1):
            growth = jnp.exp(wave * source[s])
            values = fields(s)
            scaled = [growth * value for value in values]
            prefix = [a + b for a, b in zip(prefix, scaled)]
            moment = [a + source[s] * b for a, b in zip(moment, scaled)]
            if s % 2 == 0:
                r = s // 2
                z = receiver[r]
                fall, rise = jnp.exp(-wave * z), jnp.exp(wave * z)
                summed, slope = [], []
                for n in range(4):
                    after, after_moment = suffix_ref[r, n, 0:rows, :], suffix_ref[r, 4 + n, 0:rows, :]
                    summed.append(fall * (prefix[n] + total[n]) + rise * after)
                    slope.append(
                        wave
                        * (
                            fall * (z * (prefix[n] - total[n]) - (moment[n] + total_moment[n]))
                            + rise * (after_moment - z * after)
                        )
                    )
                weight = row_weight * rigidity[r]
                along = [a - b for a, b in zip(summed, slope)]
                write(
                    r,
                    [
                        weight * (summed[0] - uu * slope[0] - uv * slope[2]),
                        weight * (summed[1] - uu * slope[1] - uv * slope[3]),
                        weight * (summed[2] - uv * slope[0] - vv * slope[2]),
                        weight * (summed[3] - uv * slope[1] - vv * slope[3]),
                        -weight * friction[r] * (odd_x * along[1] + odd_y * along[3]),
                        weight * friction[r] * (odd_x * along[0] + odd_y * along[2]),
                    ],
                )

    for half in range(2):

        def write_edge(r, values):
            for n in range(6):
                edge_ref[r, n] = values[n] * only_first

        unit(4, 256, 4, half, jnp.full((4, 128), -HALF, jnp.int32), jnp.ones((4, 128), F32), write_edge)

        def write_main(r, values):
            for c in range(3):
                real, imag = values[2 * c], values[2 * c + 1]
                pad = jnp.zeros((4, 128), F32)
                real = real - jnp.concatenate([edge_ref[r, 2 * c + 1], pad], axis=0)
                imag = imag + jnp.concatenate([edge_ref[r, 2 * c], pad], axis=0)
                place = pl.ds(64 * c + r, 8, stride=8)
                trac_ref.at[half][place, :] = real
                trac_ref.at[2 + half][place, :] = -imag

        kind = lax.broadcasted_iota(jnp.int32, (8, 128), 0) // 4
        weight = jnp.where(kind == 0, 1.0 + keep_imag, 2.0).astype(F32)
        unit(8, 0, 8, half, 2 * j + kind, weight, write_main)

    high, low = halves(jnp.concatenate([trac_ref[t] for t in range(4)], axis=1))
    turned = dot(high, table_ref[0]) + dot(low, table_ref[0]) + dot(high, table_ref[1])
    for c in range(3):
        fields = []
        for p in range(2):
            items = []
            for k0 in range(4):
                row = 64 * c + 32 * p + 8 * k0
                items.append(times((turned[row : row + 8, :256], turned[row : row + 8, 256:]), cosines[k0], sines[k0]))
            mixed = radix_four(items)
            fields.append([item[0] for item in mixed])
            fields.append([-item[1] for item in mixed])
        for outer in range(8):
            cut = slice(128 * (outer % 2), 128 * (outer % 2) + 128)
            group = swap_groups([fields[n][outer // 2][:, cut] for n in range(4)])
            for inner in range(4):
                w = 4 * outer + inner
                out_ref[pl.ds(24 * w + c, 8, stride=3), :] = group[inner]


def inverse_rows(table_ref, got_ref, out_ref):
    flipped = [got_ref[pl.ds(c, DEVICES, stride=3), :].T for c in range(3)]
    parts = []
    for parity in range(2):
        rows = []
        for c in range(3):
            real = flipped[c][64 * parity : 64 * parity + 32]
            imag = flipped[c][64 * parity + 32 : 64 * parity + 64]
            rows.append(jnp.concatenate([real, imag], axis=1))
        high, low = halves(jnp.concatenate(rows, axis=0))
        part = slice(parity * HALF, (parity + 1) * HALF)
        parts.append(
            dot(high, table_ref[0, part]) + dot(low, table_ref[0, part]) + dot(high, table_ref[1, part])
        )
    for side, stress in enumerate((parts[0] + parts[1], parts[0] - parts[1])):
        first, second, third = stress[0:32], stress[32:64], stress[64:96]
        out_ref[:, side * HALF : (side + 1) * HALF] = jnp.sqrt(first * first + second * second + 1.0) + third


def spec(space=VMEM):
    return pl.BlockSpec(memory_space=space)


def run_forward(mask, slip, table, interpret=False):
    return pl.pallas_call(
        forward_rows,
        out_shape=jax.ShapeDtypeStruct((4 * DEVICES, 128), F32),
        in_specs=[spec()] * 3,
        out_specs=spec(),
        interpret=interpret,
        name="forward_rows",
    )(mask, slip, table)


def run_middle(position, slice_layer, layer_material, materials, table, twiddle, got, interpret=False):
    return pl.pallas_call(
        functools.partial(middle, position),
        out_shape=jax.ShapeDtypeStruct((3 * DEVICES, 128), F32),
        in_specs=[spec(SMEM)] * 3 + [spec()] * 3,
        out_specs=spec(),
        scratch_shapes=[
            VMEM((4, 384, 128), F32),
            VMEM((384, 512), F32),
            VMEM((R, 6, 4, 128), F32),
            VMEM((R, 8, 8, 128), F32),
            VMEM((4, 192, 128), F32),
        ],
        interpret=interpret,
        name="middle",
    )(slice_layer, layer_material, materials, table, twiddle, got)


def run_inverse(table, got, interpret=False):
    return pl.pallas_call(
        inverse_rows,
        out_shape=jax.ShapeDtypeStruct((32, GRID), F32),
        in_specs=[spec()] * 2,
        out_specs=spec(),
        interpret=interpret,
        name="inverse_rows",
    )(table, got)


def exchange(rows):
    blocks = rows.reshape((DEVICES, rows.shape[0] // DEVICES, 128))
    moved = lax.all_to_all(blocks, ("wave", "depth"), split_axis=0, concat_axis=0, tiled=True)
    return moved.reshape(rows.shape)


def shards(slip_field, slip_mask, slice_layer, layer_material, materials):
    real_dft, complex_dft, twiddle = tables()

    def position():
        return lax.axis_index("wave") * lax.axis_size("depth") + lax.axis_index("depth")

    sent = run_forward(slip_mask.reshape((2, 32)), slip_field.reshape((128, GRID)), real_dft)
    half = run_middle(
        position, slice_layer, layer_material, materials.reshape((24,)), complex_dft, twiddle, exchange(sent)
    )
    return run_inverse(real_dft, exchange(half)).reshape((1, 32, GRID))


def solution(mesh):
    placed = (P("depth", None, "wave", None), P("depth", "wave", None), P(), P(), P())
    return jax.shard_map(
        shards, mesh=mesh, in_specs=placed, out_specs=P("depth", "wave", None), check_vma=False
    )
```

time: 482 us -> 78 us (0.16); the launches traced: 476 us -> 77.7 us
  matrix products: 146 us -> 0 us
  waiting for transfers between devices: 102 us -> 20 us
  local copies, waits for them, and re-layouts: 83.1 us -> 3.48 us
  other arithmetic: 50.4 us -> 0 us
  loops' own time: 43 us -> 0 us
  blocking collectives: 0 us -> 26.9 us
  starting transfers between devices: 37 us -> 15.6 us
  between operations: 14.2 us -> 0.02 us
  Pallas kernels: 0 us -> 11.7 us
    dot_general x29 -> x0, matrix products: 146 us -> none  [the longest x7 44.4 us: complex_einsum(): second = jnp.einsum(einsum_form, real_part, sine_part, precision=highest)]
    all_gather x2 -> x0, waiting for transfers between devices: 98.3 us -> none  [the longest x1 59.2 us: shards(): lax.all_gather(spec_real, 'depth', axis=0, tiled=True)]
    another operation x1 -> x0, loops' own time: 43 us -> none  [contract(): return lax.fori_loop(0, spec_real.shape[0], add_source, totals)]
    all_to_all x0 -> x1, blocking collectives: none -> 26.9 us  [exchange(): lax.all_to_all(blocks, ('wave', 'depth'), split_axis=0, concat_axis=0, ti...]
    add x33 -> x0, other arithmetic: 25.3 us -> none  [the longest x16 21.1 us: add_source(): strike * first_imag + cross_term * second_imag]
    unnamed x54 -> x4, local copies, waits for them, and re-layouts: 26 us -> 0.79 us
    all_to_all x4 -> x1, starting transfers between devices: 36.5 us -> 15.6 us  [exchange(): lax.all_to_all(blocks, ('wave', 'depth'), split_axis=0, concat_axis=0, ti...]
    mul x9 -> x0, local copies, waits for them, and re-layouts: 19.5 us -> none  [the longest x3 9.01 us: transform_last(): final_imag.reshape(leading + (length,)) * norm_scale]
  transfers between devices with their start and end apart: 6 -> 1, of which waited for: 4 -> 1; matrix products, arithmetic and copies ran while one was open for 21% -> 1% of each run, Pallas kernels for 0% -> 0%
where the time goes in v1:
time: 78 us; the launch traced here: 77.7 us
  blocking collectives  26.9 us (34%)
  waiting for transfers between devices  20 us (26%)
  starting transfers between devices  15.6 us (20%)
  Pallas kernels  11.7 us (15%)
  local copies, waits for them, and re-layouts  3.48 us (4%)
    all_to_all x1, blocking collectives, exchange(): lax.all_to_all(blocks, ('wave', 'depth'), split_axis=0, concat_axis=0, ti...  26.9 us
    all_to_all x1, waiting for transfers between devices, exchange(): lax.all_to_all(blocks, ('wave', 'depth'), split_axis=0, concat_axis=0, ti...  20 us
    all_to_all x1, starting transfers between devices, exchange(): lax.all_to_all(blocks, ('wave', 'depth'), split_axis=0, concat_axis=0, ti...  15.6 us
    pallas_call x1, Pallas kernels, run_middle(): pl.pallas_call(functools.partial(middle, position), out_shape=jax.ShapeDt...  4.95 us
    pallas_call x1, Pallas kernels, run_forward(): pl.pallas_call(forward_rows, out_shape=jax.ShapeDtypeStruct((4 * DEVICES,...  3.64 us
    pallas_call x1, Pallas kernels, run_inverse(): pl.pallas_call(inverse_rows, out_shape=jax.ShapeDtypeStruct((32, GRID), F...  3.09 us
  transfers between devices with their start and end apart: 1, of which 1 were waited for; matrix products, arithmetic and copies ran while one was open for 1% of the time, Pallas kernels for 0%

profile of v1, /device:TPU:1, one launch (start us, length us, event | category | flops | bytes accessed | tf_op | source)
XLA Modules:
  0.0 77.7 jit_solution(16943838771241547268)
XLA Ops:
  0.0 0.0 copy-start.1
  0.0 3.6 %forward_rows.1 = f32[1024,128]{1,0:T(8,128)} custom-call(s32[2,32]{1,0:T(2,128)} %bitcast.8, bf16[128,1024]{1,0:T(8,128)(2,1)} %bitcast.7, bf16[2,1024,512]{2,1,0:T(8,128)(2,1)} %constant.6.clone.table_ref), custom_call_target="tpu_custom_call" | custom-call | tf_op jit(solution)/shard_map/forward_rows/pallas_call | solution.py:334
  3.6 15.6 %all-to-all-start = ((f32[256,4,128]{2,1,0:T(4,128)}), f32[256,4,128]{2,1,0:T(4,128)S(1)}, u32[]{:S(2)}, u32[]{:S(2)}) async-start(f32[256,4,128]{2,1,0:T(4,128)} %bitcast.6), calls=%async_computation | async-start | bytes 1048576 | tf_op jit(solution)/shard_map/all_to_all | solution.py:375
  19.3 0.0 copy-done.1
  19.3 0.6 reshape.24.material_ref
  19.9 20.0 %all-to-all-done = f32[256,4,128]{2,1,0:T(4,128)S(1)} async-done(((f32[256,4,128]{2,1,0:T(4,128)}), f32[256,4,128]{2,1,0:T(4,128)S(1)}, u32[]{:S(2)}, u32[]{:S(2)}) %all-to-all-start) | async-done | bytes 524320 | tf_op jit(solution)/shard_map/all_to_all | solution.py:375
  39.9 0.0 copy-start
  39.9 0.8 %copy-done = f32[256,4,128]{2,1,0:T(4,128)} copy-done((f32[256,4,128]{2,1,0:T(4,128)}, f32[256,4,128]{2,1,0:T(4,128)S(1)}, u32[]{:S(2)}) %copy-start) | copy-done | bytes 524312
  40.6 5.0 %middle.1 = f32[768,128]{1,0:T(8,128)} custom-call(s32[64]{0:T(128)} %slice_ref.1, s32[16]{0:T(128)} %layer_ref.1, f32[24]{0:T(128)} %reshape.24.material_ref, bf16[2,512,512]{2,1,0:T(8,128)(2,1)} %constant.7.clone.table_ref, f32[8,256]{1,0:T(8,128)} %constant.8.clone.twiddle_ref, f32[1024,128]{1,0:T(8,128)} %bitcast.5), custom_call_target="tpu_custom_call" | custom-call | tf_op jit(solution)/shard_map/middle/pallas_call | solution.py:345
  45.6 1.2 %reshape.29 = f32[256,3,128]{2,1,0:T(4,128)S(1)} reshape(f32[768,128]{1,0:T(8,128)} %middle.1) | data formatting | bytes 786432 | tf_op jit(solution)/shard_map/reshape | solution.py:374
  46.8 26.9 %all_to_all.10 = f32[256,3,128]{2,1,0:T(4,128)S(1)} all-to-all(f32[256,3,128]{2,1,0:T(4,128)S(1)} %reshape.29), channel_id=1, replica_groups=mesh['wave'=32,'depth'=8] {'wave','depth'}, dimensions={0} | all-to-all | bytes 786432 | tf_op jit(solution)/shard_map/all_to_all | solution.py:375
  73.7 0.9 %reshape.30.got_ref = f32[768,128]{1,0:T(8,128)} reshape(f32[256,3,128]{2,1,0:T(4,128)S(1)} %all_to_all.10) | data formatting | bytes 786432 | tf_op jit(solution)/shard_map/reshape | solution.py:376
  74.6 3.1 %inverse_rows.1 = f32[32,1024]{1,0:T(8,128)} custom-call(bf16[2,1024,512]{2,1,0:T(8,128)(2,1)} %constant.6.clone.table_ref, f32[768,128]{1,0:T(8,128)} %reshape.30.got_ref), custom_call_target="tpu_custom_call" | custom-call | tf_op jit(solution)/shard_map/inverse_rows/pallas_call | solution.py:363
Async XLA Ops:
  0.0 19.3 %copy-start.1 = (f32[3,8]{1,0:T(4,128)S(1)}, f32[3,8]{1,0:T(4,128)}, u32[]{:S(2)}) copy-start(f32[3,8]{1,0:T(4,128)} %param.12) | copy-start | bytes 292
  3.6 36.2 %all-to-all-start = ((f32[256,4,128]{2,1,0:T(4,128)}), f32[256,4,128]{2,1,0:T(4,128)S(1)}, u32[]{:S(2)}, u32[]{:S(2)}) async-start(f32[256,4,128]{2,1,0:T(4,128)} %bitcast.6), calls=%async_computation | async-start | bytes 1048576 | tf_op jit(solution)/shard_map/all_to_all | solution.py:375
  39.9 0.8 %copy-start = (f32[256,4,128]{2,1,0:T(4,128)}, f32[256,4,128]{2,1,0:T(4,128)S(1)}, u32[]{:S(2)}) copy-start(f32[256,4,128]{2,1,0:T(4,128)S(1)} %all-to-all-done) | copy-start | bytes 1572868

commit v2 on v1

--- a/solution.py
+++ b/solution.py
@@ -150,10 +150,8 @@
 
 
 def middle(
-    position,
-    slice_ref,
-    layer_ref,
-    material_ref,
+    j,
+    columns,
     table_ref,
     twiddle_ref,
     got_ref,
@@ -164,9 +162,8 @@
     suffix_ref,
     trac_ref,
 ):
-    j = position()
     first = j == 0
-    source, receiver, rigidity, friction = depths(slice_ref, layer_ref, material_ref)
+    source, receiver, rigidity, friction = columns
     keep_imag = jnp.where(first, 0.0, 1.0).astype(F32)
     only_first = 1.0 - keep_imag
     cosines = [twiddle_ref[a : a + 1, :] for a in range(4)]
@@ -304,11 +301,11 @@
             group = swap_groups([fields[n][outer // 2][:, cut] for n in range(4)])
             for inner in range(4):
                 w = 4 * outer + inner
-                out_ref[pl.ds(24 * w + c, 8, stride=3), :] = group[inner]
+                out_ref[pl.ds(32 * w + c, 8, stride=4), :] = group[inner]
 
 
 def inverse_rows(table_ref, got_ref, out_ref):
-    flipped = [got_ref[pl.ds(c, DEVICES, stride=3), :].T for c in range(3)]
+    flipped = [got_ref[pl.ds(c, DEVICES, stride=4), :].T for c in range(3)]
     parts = []
     for parity in range(2):
         rows = []
@@ -326,67 +323,163 @@
         out_ref[:, side * HALF : (side + 1) * HALF] = jnp.sqrt(first * first + second * second + 1.0) + third
 
 
+NEAR = (4, 3, 5, 2, 6, 1, 7, 0)
+MESH = pl.DeviceIdType.MESH
+
+
+def fused(
+    mask_ref,
+    slip_ref,
+    slice_ref,
+    layer_ref,
+    material_ref,
+    twiddle_ref,
+    real_hbm,
+    complex_hbm,
+    out_ref,
+    real_ref,
+    complex_ref,
+    rows_ref,
+    sent_ref,
+    got_ref,
+    send_ref,
+    take_ref,
+    left_ref,
+    spec_ref,
+    edge_ref,
+    suffix_ref,
+    trac_ref,
+    table_sem,
+    copy_sem,
+    send_sem,
+    take_sem,
+    ready_sem,
+):
+    w, d = lax.axis_index("wave"), lax.axis_index("depth")
+    me = w * 8 + d
+    z, low, core = w // 4, (w // 2) % 2, w % 2
+    high, y = d // 4, d % 4
+    x = 2 * high + low
+    rings = [((z + n) % 8) * 4 for n in range(8)]
+    cores = [core, 1 - core]
+
+    real_copy = pltpu.make_async_copy(real_hbm, real_ref, table_sem.at[0])
+    complex_copy = pltpu.make_async_copy(complex_hbm, complex_ref, table_sem.at[1])
+    real_copy.start()
+    complex_copy.start()
+
+    def greet(sem, pillar):
+        for n in range(1, 16):
+            if pillar:
+                other = 2 * low if n < 8 else 2 - 2 * low
+                place = (rings[n % 8] + other + core, d)
+            else:
+                side = 4 * high if (n // 2) % 2 == 0 else 4 - 4 * high
+                place = (4 * z + 2 * low + cores[n % 2], side + (y + n // 4) % 4)
+            pl.semaphore_signal(sem, 1, device_id=place, device_id_type=MESH)
+
+    barrier = pltpu.get_barrier_semaphore()
+    greet(barrier, True)
+    greet(barrier, False)
+    real_copy.wait()
+    forward_rows(mask_ref, slip_ref, real_ref, rows_ref)
+    sent_ref[...] = rows_ref[...].reshape(sent_ref.shape)
+    pl.semaphore_wait(barrier, 30)
+    greet(ready_sem, True)
+    pl.semaphore_wait(ready_sem, 15)
+
+    def exchange(source, target, number):
+        def send(w_base, d_to, skip):
+            for n in NEAR:
+                for c in (1, 0):
+                    if skip and n == 0 and c == 0:
+                        continue
+                    w_to = w_base + rings[n] + cores[c]
+                    pltpu.make_async_remote_copy(
+                        source.at[w_to * 8 + d_to],
+                        target.at[me],
+                        send_sem.at[number],
+                        take_sem.at[number],
+                        device_id=(w_to, d_to),
+                        device_id_type=MESH,
+                    ).start()
+
+        def sheet(n, carry):
+            order = (n + 11) % 16
+            y_to, x_to = (y + order // 4 + 2) % 4, (x + order + 2) % 4
+            send((x_to % 2) * 2, (x_to // 2) * 4 + y_to, False)
+            return carry
+
+        lax.fori_loop(0, 15, sheet, 0)
+        send(2 * low, d, True)
+        own = pltpu.make_async_copy(source.at[me], target.at[me], copy_sem.at[number])
+        own.start()
+        return own
+
+    def finish(own, source, target, number):
+        own.wait()
+        most = pl.ds(0, DEVICES - 1)
+        pltpu.make_async_copy(source.at[most], target.at[most], send_sem.at[number]).wait()
+        pltpu.make_async_copy(source.at[most], target.at[most], take_sem.at[number]).wait()
+
+    own = exchange(sent_ref, got_ref, 0)
+    columns = depths(slice_ref, layer_ref, material_ref)
+    complex_copy.wait()
+    finish(own, sent_ref, got_ref, 0)
+    rows_ref[...] = got_ref[...].reshape(rows_ref.shape)
+    middle(
+        me, columns, complex_ref, twiddle_ref, rows_ref, rows_ref, left_ref, spec_ref, edge_ref, suffix_ref, trac_ref
+    )
+    send_ref[...] = rows_ref[...].reshape(send_ref.shape).astype(BF16)
+    own = exchange(send_ref, take_ref, 1)
+    finish(own, send_ref, take_ref, 1)
+    rows_ref[...] = take_ref[...].astype(F32).reshape(rows_ref.shape)
+    inverse_rows(real_ref, rows_ref, out_ref)
+
+
 def spec(space=VMEM):
     return pl.BlockSpec(memory_space=space)
 
 
-def run_forward(mask, slip, table, interpret=False):
-    return pl.pallas_call(
-        forward_rows,
-        out_shape=jax.ShapeDtypeStruct((4 * DEVICES, 128), F32),
-        in_specs=[spec()] * 3,
-        out_specs=spec(),
-        interpret=interpret,
-        name="forward_rows",
-    )(mask, slip, table)
-
-
-def run_middle(position, slice_layer, layer_material, materials, table, twiddle, got, interpret=False):
-    return pl.pallas_call(
-        functools.partial(middle, position),
-        out_shape=jax.ShapeDtypeStruct((3 * DEVICES, 128), F32),
-        in_specs=[spec(SMEM)] * 3 + [spec()] * 3,
+def shards(slip_field, slip_mask, slice_layer, layer_material, materials):
+    real_dft, complex_dft, twiddle = tables()
+    result = pl.pallas_call(
+        fused,
+        out_shape=jax.ShapeDtypeStruct((32, GRID), F32),
+        in_specs=[spec()] * 2 + [spec(SMEM)] * 3 + [spec()] + [spec(pl.ANY)] * 2,
         out_specs=spec(),
         scratch_shapes=[
+            VMEM((2, GRID, HALF), BF16),
+            VMEM((2, HALF, HALF), BF16),
+            VMEM((4 * DEVICES, 128), F32),
+            VMEM((DEVICES, 4, 128), F32),
+            VMEM((DEVICES, 4, 128), F32),
+            VMEM((DEVICES, 4, 128), BF16),
+            VMEM((DEVICES, 4, 128), BF16),
             VMEM((4, 384, 128), F32),
             VMEM((384, 512), F32),
             VMEM((R, 6, 4, 128), F32),
             VMEM((R, 8, 8, 128), F32),
             VMEM((4, 192, 128), F32),
+            pltpu.SemaphoreType.DMA((2,)),
+            pltpu.SemaphoreType.DMA((2,)),
+            pltpu.SemaphoreType.DMA((2,)),
+            pltpu.SemaphoreType.DMA((2,)),
+            pltpu.SemaphoreType.REGULAR,
         ],
-        interpret=interpret,
-        name="middle",
-    )(slice_layer, layer_material, materials, table, twiddle, got)
-
-
-def run_inverse(table, got, interpret=False):
-    return pl.pallas_call(
-        inverse_rows,
-        out_shape=jax.ShapeDtypeStruct((32, GRID), F32),
-        in_specs=[spec()] * 2,
-        out_specs=spec(),
-        interpret=interpret,
-        name="inverse_rows",
-    )(table, got)
-
-
-def exchange(rows):
-    blocks = rows.reshape((DEVICES, rows.shape[0] // DEVICES, 128))
-    moved = lax.all_to_all(blocks, ("wave", "depth"), split_axis=0, concat_axis=0, tiled=True)
-    return moved.reshape(rows.shape)
-
-
-def shards(slip_field, slip_mask, slice_layer, layer_material, materials):
-    real_dft, complex_dft, twiddle = tables()
-
-    def position():
-        return lax.axis_index("wave") * lax.axis_size("depth") + lax.axis_index("depth")
-
-    sent = run_forward(slip_mask.reshape((2, 32)), slip_field.reshape((128, GRID)), real_dft)
-    half = run_middle(
-        position, slice_layer, layer_material, materials.reshape((24,)), complex_dft, twiddle, exchange(sent)
+        compiler_params=pltpu.CompilerParams(collective_id=0, has_side_effects=True),
+        name="fused",
+    )(
+        slip_mask.reshape((2, 32)),
+        slip_field.reshape((128, GRID)),
+        slice_layer,
+        layer_material,
+        materials.reshape((24,)),
+        twiddle,
+        real_dft,
+        complex_dft,
     )
-    return run_inverse(real_dft, exchange(half)).reshape((1, 32, GRID))
+    return result.reshape((1, 32, GRID))
 
 
 def solution(mesh):

time: 78 us -> 47.4 us (0.61)
  Pallas kernels: 11.7 us -> 44.4 us
  blocking collectives: 26.9 us -> 0 us
  waiting for transfers between devices: 20 us -> 0 us
  starting transfers between devices: 15.6 us -> 0 us
    pallas_call x3 -> x1, Pallas kernels: 11.7 us -> 44.4 us  [shards(): pl.pallas_call(fused, out_shape=jax.ShapeDtypeStruct((32, GRID), F32), in...]
    all_to_all x1 -> x0, blocking collectives: 26.9 us -> none  [exchange(): lax.all_to_all(blocks, ('wave', 'depth'), split_axis=0, concat_axis=0, ti...]
    all_to_all x1 -> x0, waiting for transfers between devices: 20 us -> none  [exchange(): lax.all_to_all(blocks, ('wave', 'depth'), split_axis=0, concat_axis=0, ti...]
    all_to_all x1 -> x0, starting transfers between devices: 15.6 us -> none  [exchange(): lax.all_to_all(blocks, ('wave', 'depth'), split_axis=0, concat_axis=0, ti...]
    reshape x2 -> x0, local copies, waits for them, and re-layouts: 2.09 us -> none  [the longest x1 1.16 us: exchange(): blocks = rows.reshape((DEVICES, rows.shape[0] // DEVICES, 128))]
    unnamed x4 -> x1, local copies, waits for them, and re-layouts: 0.79 us -> 1.57 us
  transfers between devices with their start and end apart: 1 -> 0, of which waited for: 1 -> 0; matrix products, arithmetic and copies ran while one was open for 1% -> 0% of each run, Pallas kernels for 0% -> 0%
where the time goes in v2:
time: 47.4 us; the launch traced here: 47.3 us
  Pallas kernels  44.4 us (94%)
  local copies, waits for them, and re-layouts  2.84 us (6%)
    pallas_call x1, Pallas kernels, shards(): pl.pallas_call(fused, out_shape=jax.ShapeDtypeStruct((32, GRID), F32), in...  44.4 us
    unnamed x1, local copies, waits for them, and re-layouts  1.57 us
    reshape x1, local copies, waits for them, and re-layouts, shards(): materials.reshape((24,))  1.27 us

profile of v2, /device:TPU:1, one launch (start us, length us, event | category | flops | bytes accessed | tf_op | source)
XLA Modules:
  0.0 47.3 jit_solution(4718791816747339167)
XLA Ops:
  0.0 1.3 %reshape.14.material_ref = f32[24]{0:T(128)} reshape(f32[3,8]{1,0:T(4,128)} %param.12) | data formatting | bytes 192 | tf_op jit(solution)/shard_map/reshape | solution.py:477
  1.3 44.4 %fused.1 = f32[32,1024]{1,0:T(8,128)} custom-call(s32[2,32]{1,0:T(2,128)} %bitcast.5, bf16[128,1024]{1,0:T(8,128)(2,1)} %bitcast.4, s32[64]{0:T(128)} %slice_ref.1, s32[16]{0:T(128)} %layer_ref.1, f32[24]{0:T(128)} %reshape.14.material_ref, f32[8,256]{1,0:T(8,128)} %constant.6.clone.twiddle_ref, bf16[2,1024,512]{2,1,0:T(8,128)(2,1)} %constant.7.clone.real_hbm, ...), custom_call_target="tpu_custom_call" | custom-call | tf_op jit(solution)/shard_map/fused/pallas_call | solution.py:446
  45.7 1.6 %copy.10 = f32[1,32,1024]{2,1,0:T(8,128)} copy(f32[1,32,1024]{2,1,0:T(8,128)} %bitcast.3) | data formatting | bytes 262144

commit v3 on v2

--- a/solution.py
+++ b/solution.py
@@ -17,6 +17,8 @@
 R = 8
 NZ = 64
 DEVICES = 256
+LARGEST = 6.0 * GRID / 32.0
+CODE_SCALE = 32700.0 / LARGEST**0.25
 BF16 = jnp.bfloat16
 F32 = jnp.float32
 VMEM = pltpu.VMEM
@@ -77,9 +79,9 @@
             + dot(table_ref[1, part], high, True)
         )
         for imag in range(2):
-            out_ref[pl.ds(2 * parity + imag, QUARTER, stride=4), :] = result[
-                imag * QUARTER : (imag + 1) * QUARTER
-            ]
+            out_ref[pl.ds(2 * parity + imag, QUARTER, stride=4), :] = encode(
+                result[imag * QUARTER : (imag + 1) * QUARTER]
+            )
 
 
 def swap_groups(items):
@@ -99,6 +101,15 @@
     return items
 
 
+def encode(value):
+    code = jnp.sqrt(jnp.sqrt(jnp.abs(value))) * CODE_SCALE + 0.5
+    return jnp.where(value < 0.0, -code, code)
+
+
+def decode(code):
+    return (code * jnp.abs(code)) * (code * code) * (1.0 / CODE_SCALE) ** 4
+
+
 def radix_four(items):
     (r0, i0), (r1, i1), (r2, i2), (r3, i3) = items
     ar, ai, br, bi = r0 + r2, i0 + i2, r0 - r2, i0 - i2
@@ -121,32 +132,47 @@
     top = None
     for place in range(NZ):
         kind = layer_ref[slice_ref[place]]
-        thickness = jnp.float32(0.1) * material_ref[kind]
+        thickness = jnp.float32(0.1) * material_ref[0, kind]
         top = thickness if top is None else top + thickness
         center.append(top - 0.5 * thickness)
         if place % 8 == 3:
-            rigidity.append(material_ref[8 + kind])
-            friction.append(material_ref[16 + kind])
+            rigidity.append(material_ref[1, kind])
+            friction.append(material_ref[2, kind])
     source = [center[4 * s + 1] for s in range(S)]
     receiver = [center[8 * r + 3] for r in range(R)]
     return source, receiver, rigidity, friction
 
 
-def geometry(first_row, rows, half, ky):
-    k0 = lax.broadcasted_iota(jnp.int32, (rows, 128), 0) % 4
-    k1 = lax.broadcasted_iota(jnp.int32, (rows, 128), 1) + 128 * half
-    kx = 4 * k1 + k0
+def wave_arrays(sort, j):
+    row = lax.broadcasted_iota(jnp.int32, (8, 128), 0)
+    lane = lax.broadcasted_iota(jnp.int32, (8, 128), 1)
+    half = row // 4 if sort == 2 else sort
+    kx = 4 * (lane + 128 * half) + row % 4
     signed = jnp.where(kx >= HALF, kx - GRID, kx)
+    ky = jnp.full((8, 128), -HALF, jnp.int32) if sort == 2 else 2 * j + row // 4
     x_wave, y_wave = signed.astype(F32), ky.astype(F32)
     magnitude = jnp.sqrt(x_wave * x_wave + y_wave * y_wave)
     bounded = jnp.maximum(magnitude, 1.0)
     along_x, along_y = x_wave / bounded, y_wave / bounded
-    x_edge, y_edge = signed == -HALF, ky == -HALF
+    x_edge = signed == -HALF
+    y_edge = ky == -HALF
     cross = jnp.where(x_edge != y_edge, 0.0, along_x * along_y)
     odd_x = jnp.where(x_edge, 0.0, along_x)
     odd_y = jnp.where(y_edge, 0.0, along_y)
     wave = 2.0 * math.pi / GRID * magnitude
     return wave, along_x * along_x, cross, along_y * along_y, odd_x, odd_y
+
+
+def prepare(j, columns, wave_ref, grow_ref, fall_ref):
+    source, receiver = columns[0], columns[1]
+    for sort in range(3):
+        arrays = wave_arrays(sort, j)
+        for n, value in enumerate(arrays):
+            wave_ref[sort, n] = value
+        for n, z in enumerate(source + receiver):
+            exponent = arrays[0] * z
+            grow_ref[sort, n] = jnp.exp(exponent)
+            fall_ref[sort, n] = jnp.exp(-exponent)
 
 
 def middle(
@@ -158,18 +184,21 @@
     out_ref,
     left_ref,
     spec_ref,
+    rim_ref,
     edge_ref,
     suffix_ref,
     trac_ref,
+    wave_ref,
+    grow_ref,
+    fall_ref,
 ):
-    first = j == 0
     source, receiver, rigidity, friction = columns
-    keep_imag = jnp.where(first, 0.0, 1.0).astype(F32)
+    keep_imag = jnp.where(j == 0, 0.0, 1.0).astype(F32)
     only_first = 1.0 - keep_imag
     cosines = [twiddle_ref[a : a + 1, :] for a in range(4)]
     sines = [twiddle_ref[4 + a : 5 + a, :] for a in range(4)]
 
-    loaded = [got_ref[pl.ds(c, DEVICES, stride=4), :] for c in range(4)]
+    loaded = [decode(got_ref[pl.ds(c, DEVICES, stride=4), :]) for c in range(4)]
     blocks = [[[None] * 8 for _ in range(4)] for _ in range(4)]
     for c in range(4):
         for outer in range(8):
@@ -189,66 +218,71 @@
         for p in range(3):
             mixed = radix_four(kinds[p])
             for k0 in range(4):
-                real, imag = times(mixed[k0], cosines[k0], sines[k0])
+                real, imag = times(mixed[k0], cosines[k0], sines[k0]) if k0 else mixed[k0]
                 if p < 2:
                     place = pl.ds(64 * g + 4 * p + k0, 8, stride=8)
                 else:
-                    place = pl.ds(256 + 32 * g + k0, 8, stride=4)
+                    place = pl.ds(256 + 32 * k0 + 8 * g, 8)
                 for t in range(2):
                     left_ref.at[t][place, :] = real[:, 128 * t : 128 * t + 128]
                     left_ref.at[2 + t][place, :] = imag[:, 128 * t : 128 * t + 128]
     high, low = halves(jnp.concatenate([left_ref[t] for t in range(4)], axis=1))
     spectra = dot(high, table_ref[0]) + dot(low, table_ref[0]) + dot(high, table_ref[1])
-    spec_ref[...] = spectra.astype(BF16).astype(F32)
-
-    def unit(rows, base, step, half, ky, row_weight, write):
-        wave, uu, uv, vv, odd_x, odd_y = geometry(0, rows, half, ky)
+    spectra = spectra.astype(BF16).astype(F32)
+    spec_ref[...] = spectra[:256]
+    for k0 in range(4):
+        for t in range(4):
+            rows = spectra[256 + 32 * k0 : 288 + 32 * k0, 128 * t : 128 * t + 128]
+            rim_ref.at[t // 2][pl.ds(4 * (t % 2) + k0, 32, stride=8), :] = rows
+
+    def unit(sort, row_weight, write):
+        wave, uu, uv, vv, odd_x, odd_y = [wave_ref[sort, n] for n in range(6)]
 
         def fields(s):
             picked = []
             for q in range(2):
-                row = base + (2 * (s % 2) + q) * 8 * step + (s // 2) * step
+                row = 8 * ((2 * (s % 2) + q) * 8 + s // 2)
                 for imag in range(2):
-                    start = 256 * imag + 128 * half
-                    picked.append(spec_ref[row : row + rows, start : start + 128])
+                    if sort == 2:
+                        picked.append(rim_ref[imag, row : row + 8, :])
+                    else:
+                        start = 256 * imag + 128 * sort
+                        picked.append(spec_ref[row : row + 8, start : start + 128])
             return picked
 
-        zero = jnp.zeros((rows, 128), F32)
+        zero = jnp.zeros((8, 128), F32)
         suffix, moment = [zero] * 4, [zero] * 4
         for s in reversed(range(S)):
-            decay = jnp.exp(-wave * source[s])
-            values = fields(s)
-            scaled = [decay * value for value in values]
+            decay = fall_ref[sort, s]
+            scaled = [decay * value for value in fields(s)]
             suffix = [a + b for a, b in zip(suffix, scaled)]
             moment = [a + source[s] * b for a, b in zip(moment, scaled)]
             if s % 2 == 1:
                 for n in range(4):
-                    suffix_ref[s // 2, n, 0:rows, :] = suffix[n]
-                    suffix_ref[s // 2, 4 + n, 0:rows, :] = moment[n]
+                    suffix_ref[s // 2, n] = suffix[n]
+                    suffix_ref[s // 2, 4 + n] = moment[n]
         total, total_moment = suffix, moment
         prefix, moment = [zero] * 4, [zero] * 4
         for s in range(S - 1):
-            growth = jnp.exp(wave * source[s])
-            values = fields(s)
-            scaled = [growth * value for value in values]
+            growth = grow_ref[sort, s]
+            scaled = [growth * value for value in fields(s)]
             prefix = [a + b for a, b in zip(prefix, scaled)]
             moment = [a + source[s] * b for a, b in zip(moment, scaled)]
             if s % 2 == 0:
                 r = s // 2
                 z = receiver[r]
-                fall, rise = jnp.exp(-wave * z), jnp.exp(wave * z)
+                fall, rise = fall_ref[sort, S + r], grow_ref[sort, S + r]
+                wave_fall, wave_rise = wave * fall, wave * rise
                 summed, slope = [], []
                 for n in range(4):
-                    after, after_moment = suffix_ref[r, n, 0:rows, :], suffix_ref[r, 4 + n, 0:rows, :]
+                    after, after_moment = suffix_ref[r, n], suffix_ref[r, 4 + n]
                     summed.append(fall * (prefix[n] + total[n]) + rise * after)
                     slope.append(
-                        wave
-                        * (
-                            fall * (z * (prefix[n] - total[n]) - (moment[n] + total_moment[n]))
-                            + rise * (after_moment - z * after)
-                        )
+                        wave_fall * (z * (prefix[n] - total[n]) - (moment[n] + total_moment[n]))
+                        + wave_rise * (after_moment - z * after)
                     )
                 weight = row_weight * rigidity[r]
+                tilt = weight * friction[r]
                 along = [a - b for a, b in zip(summed, slope)]
                 write(
                     r,
@@ -257,32 +291,31 @@
                         weight * (summed[1] - uu * slope[1] - uv * slope[3]),
                         weight * (summed[2] - uv * slope[0] - vv * slope[2]),
                         weight * (summed[3] - uv * slope[1] - vv * slope[3]),
-                        -weight * friction[r] * (odd_x * along[1] + odd_y * along[3]),
-                        weight * friction[r] * (odd_x * along[0] + odd_y * along[2]),
+                        -tilt * (odd_x * along[1] + odd_y * along[3]),
+                        tilt * (odd_x * along[0] + odd_y * along[2]),
                     ],
                 )
 
+    def write_edge(r, values):
+        for n in range(6):
+            edge_ref[r, n] = values[n]
+
+    unit(2, only_first, write_edge)
+    kind = lax.broadcasted_iota(jnp.int32, (8, 128), 0) // 4
+    weight = jnp.where(kind == 0, 1.0 + keep_imag, 2.0).astype(F32)
+    pad = jnp.zeros((4, 128), F32)
     for half in range(2):
-
-        def write_edge(r, values):
-            for n in range(6):
-                edge_ref[r, n] = values[n] * only_first
-
-        unit(4, 256, 4, half, jnp.full((4, 128), -HALF, jnp.int32), jnp.ones((4, 128), F32), write_edge)
 
         def write_main(r, values):
             for c in range(3):
-                real, imag = values[2 * c], values[2 * c + 1]
-                pad = jnp.zeros((4, 128), F32)
-                real = real - jnp.concatenate([edge_ref[r, 2 * c + 1], pad], axis=0)
-                imag = imag + jnp.concatenate([edge_ref[r, 2 * c], pad], axis=0)
+                edges = [
+                    jnp.concatenate([edge_ref[r, 2 * c + n, 4 * half : 4 * half + 4, :], pad], axis=0) for n in range(2)
+                ]
                 place = pl.ds(64 * c + r, 8, stride=8)
-                trac_ref.at[half][place, :] = real
-                trac_ref.at[2 + half][place, :] = -imag
-
-        kind = lax.broadcasted_iota(jnp.int32, (8, 128), 0) // 4
-        weight = jnp.where(kind == 0, 1.0 + keep_imag, 2.0).astype(F32)
-        unit(8, 0, 8, half, 2 * j + kind, weight, write_main)
+                trac_ref.at[half][place, :] = values[2 * c] - edges[1]
+                trac_ref.at[2 + half][place, :] = -(values[2 * c + 1] + edges[0])
+
+        unit(half, weight, write_main)
 
     high, low = halves(jnp.concatenate([trac_ref[t] for t in range(4)], axis=1))
     turned = dot(high, table_ref[0]) + dot(low, table_ref[0]) + dot(high, table_ref[1])
@@ -292,7 +325,8 @@
             items = []
             for k0 in range(4):
                 row = 64 * c + 32 * p + 8 * k0
-                items.append(times((turned[row : row + 8, :256], turned[row : row + 8, 256:]), cosines[k0], sines[k0]))
+                item = (turned[row : row + 8, :256], turned[row : row + 8, 256:])
+                items.append(times(item, cosines[k0], sines[k0]) if k0 else item)
             mixed = radix_four(items)
             fields.append([item[0] for item in mixed])
             fields.append([-item[1] for item in mixed])
@@ -313,11 +347,9 @@
             real = flipped[c][64 * parity : 64 * parity + 32]
             imag = flipped[c][64 * parity + 32 : 64 * parity + 64]
             rows.append(jnp.concatenate([real, imag], axis=1))
-        high, low = halves(jnp.concatenate(rows, axis=0))
+        whole = jnp.concatenate(rows, axis=0).astype(BF16)
         part = slice(parity * HALF, (parity + 1) * HALF)
-        parts.append(
-            dot(high, table_ref[0, part]) + dot(low, table_ref[0, part]) + dot(high, table_ref[1, part])
-        )
+        parts.append(dot(whole, table_ref[0, part]) + dot(whole, table_ref[1, part]))
     for side, stress in enumerate((parts[0] + parts[1], parts[0] - parts[1])):
         first, second, third = stress[0:32], stress[32:64], stress[64:96]
         out_ref[:, side * HALF : (side + 1) * HALF] = jnp.sqrt(first * first + second * second + 1.0) + third
@@ -328,15 +360,21 @@
 
 
 def fused(
+    mask_hbm,
+    slip_hbm,
+    slice_hbm,
+    layer_hbm,
+    material_hbm,
+    twiddle_hbm,
+    real_hbm,
+    complex_hbm,
+    out_ref,
     mask_ref,
     slip_ref,
     slice_ref,
     layer_ref,
     material_ref,
     twiddle_ref,
-    real_hbm,
-    complex_hbm,
-    out_ref,
     real_ref,
     complex_ref,
     rows_ref,
@@ -346,10 +384,14 @@
     take_ref,
     left_ref,
     spec_ref,
+    rim_ref,
     edge_ref,
     suffix_ref,
     trac_ref,
-    table_sem,
+    wave_ref,
+    grow_ref,
+    fall_ref,
+    input_sem,
     copy_sem,
     send_sem,
     take_sem,
@@ -363,11 +405,6 @@
     rings = [((z + n) % 8) * 4 for n in range(8)]
     cores = [core, 1 - core]
 
-    real_copy = pltpu.make_async_copy(real_hbm, real_ref, table_sem.at[0])
-    complex_copy = pltpu.make_async_copy(complex_hbm, complex_ref, table_sem.at[1])
-    real_copy.start()
-    complex_copy.start()
-
     def greet(sem, pillar):
         for n in range(1, 16):
             if pillar:
@@ -381,9 +418,23 @@
     barrier = pltpu.get_barrier_semaphore()
     greet(barrier, True)
     greet(barrier, False)
-    real_copy.wait()
+    pairs = (
+        (slip_hbm, slip_ref),
+        (mask_hbm, mask_ref),
+        (real_hbm, real_ref),
+        (slice_hbm, slice_ref),
+        (layer_hbm, layer_ref),
+        (material_hbm, material_ref),
+        (twiddle_hbm, twiddle_ref),
+        (complex_hbm, complex_ref),
+    )
+    copies = [pltpu.make_async_copy(a, b, input_sem.at[n]) for n, (a, b) in enumerate(pairs)]
+    for copy in copies:
+        copy.start()
+    for copy in copies[:3]:
+        copy.wait()
     forward_rows(mask_ref, slip_ref, real_ref, rows_ref)
-    sent_ref[...] = rows_ref[...].reshape(sent_ref.shape)
+    sent_ref[...] = rows_ref[...].reshape(sent_ref.shape).astype(jnp.int32).astype(jnp.int16)
     pl.semaphore_wait(barrier, 30)
     greet(ready_sem, True)
     pl.semaphore_wait(ready_sem, 15)
@@ -423,12 +474,28 @@
         pltpu.make_async_copy(source.at[most], target.at[most], take_sem.at[number]).wait()
 
     own = exchange(sent_ref, got_ref, 0)
+    for copy in copies[3:]:
+        copy.wait()
     columns = depths(slice_ref, layer_ref, material_ref)
-    complex_copy.wait()
+    prepare(me, columns, wave_ref, grow_ref, fall_ref)
     finish(own, sent_ref, got_ref, 0)
-    rows_ref[...] = got_ref[...].reshape(rows_ref.shape)
+    rows_ref[...] = got_ref[...].astype(jnp.int32).astype(F32).reshape(rows_ref.shape)
     middle(
-        me, columns, complex_ref, twiddle_ref, rows_ref, rows_ref, left_ref, spec_ref, edge_ref, suffix_ref, trac_ref
+        me,
+        columns,
+        complex_ref,
+        twiddle_ref,
+        rows_ref,
+        rows_ref,
+        left_ref,
+        spec_ref,
+        rim_ref,
+        edge_ref,
+        suffix_ref,
+        trac_ref,
+        wave_ref,
+        grow_ref,
+        fall_ref,
     )
     send_ref[...] = rows_ref[...].reshape(send_ref.shape).astype(BF16)
     own = exchange(send_ref, take_ref, 1)
@@ -446,22 +513,32 @@
     result = pl.pallas_call(
         fused,
         out_shape=jax.ShapeDtypeStruct((32, GRID), F32),
-        in_specs=[spec()] * 2 + [spec(SMEM)] * 3 + [spec()] + [spec(pl.ANY)] * 2,
+        in_specs=[spec(pl.ANY)] * 8,
         out_specs=spec(),
         scratch_shapes=[
+            VMEM((2, 32), jnp.int32),
+            VMEM((128, GRID), BF16),
+            SMEM((NZ,), jnp.int32),
+            SMEM((16,), jnp.int32),
+            SMEM((3, 8), F32),
+            VMEM((8, QUARTER), F32),
             VMEM((2, GRID, HALF), BF16),
             VMEM((2, HALF, HALF), BF16),
             VMEM((4 * DEVICES, 128), F32),
-            VMEM((DEVICES, 4, 128), F32),
-            VMEM((DEVICES, 4, 128), F32),
+            VMEM((DEVICES, 4, 128), jnp.int16),
+            VMEM((DEVICES, 4, 128), jnp.int16),
             VMEM((DEVICES, 4, 128), BF16),
             VMEM((DEVICES, 4, 128), BF16),
             VMEM((4, 384, 128), F32),
-            VMEM((384, 512), F32),
-            VMEM((R, 6, 4, 128), F32),
+            VMEM((256, 512), F32),
+            VMEM((2, 256, 128), F32),
+            VMEM((R, 6, 8, 128), F32),
             VMEM((R, 8, 8, 128), F32),
             VMEM((4, 192, 128), F32),
-            pltpu.SemaphoreType.DMA((2,)),
+            VMEM((3, 6, 8, 128), F32),
+            VMEM((3, S + R, 8, 128), F32),
+            VMEM((3, S + R, 8, 128), F32),
+            pltpu.SemaphoreType.DMA((8,)),
             pltpu.SemaphoreType.DMA((2,)),
             pltpu.SemaphoreType.DMA((2,)),
             pltpu.SemaphoreType.DMA((2,)),
@@ -474,7 +551,7 @@
         slip_field.reshape((128, GRID)),
         slice_layer,
         layer_material,
-        materials.reshape((24,)),
+        materials,
         twiddle,
         real_dft,
         complex_dft,

time: 47.4 us -> 39.7 us (0.84)
  Pallas kernels: 44.4 us -> 38 us
  local copies, waits for them, and re-layouts: 2.84 us -> 1.57 us
    pallas_call x1, Pallas kernels: 44.4 us -> 38 us  [shards(): pl.pallas_call(fused, out_shape=jax.ShapeDtypeStruct((32, GRID), F32), in...]
    reshape x1 -> x0, local copies, waits for them, and re-layouts: 1.27 us -> none  [shards(): materials.reshape((24,))]
where the time goes in v3:
time: 39.7 us; the launch traced here: 39.6 us
  Pallas kernels  38 us (96%)
  local copies, waits for them, and re-layouts  1.57 us (4%)
    pallas_call x1, Pallas kernels, shards(): pl.pallas_call(fused, out_shape=jax.ShapeDtypeStruct((32, GRID), F32), in...  38 us
    unnamed x1, local copies, waits for them, and re-layouts  1.57 us

profile of v3, /device:TPU:1, one launch (start us, length us, event | category | flops | bytes accessed | tf_op | source)
XLA Modules:
  0.0 39.6 jit_solution(9646520687428342991)
XLA Ops:
  0.0 38.0 %fused.1 = f32[32,1024]{1,0:T(8,128)} custom-call(s32[2,32]{1,0:T(2,128)} %bitcast.5, bf16[128,1024]{1,0:T(8,128)(2,1)} %bitcast.4, s32[64]{0:T(128)} %slice_hbm.1, s32[16]{0:T(128)} %layer_hbm.1, f32[3,8]{1,0:T(4,128)} %material_hbm.1, f32[8,256]{1,0:T(8,128)} %constant.6.clone.twiddle_hbm, bf16[2,1024,512]{2,1,0:T(8,128)(2,1)} %constant.7.clone.real_hbm, ...), custom_call_target="tpu_custom_call" | custom-call | tf_op jit(solution)/shard_map/fused/pallas_call | solution.py:513
  38.0 1.6 %copy.10 = f32[1,32,1024]{2,1,0:T(8,128)} copy(f32[1,32,1024]{2,1,0:T(8,128)} %bitcast.3) | data formatting | bytes 262144

commit v4 on v3

--- a/solution.py
+++ b/solution.py
@@ -42,11 +42,11 @@
             imag[0] = 1.0 - 2.0 * (cell[0] % 2)
         rows += [real, imag]
     real_dft = np.concatenate(rows) / 32.0
-    k = np.arange(QUARTER, dtype=np.int64)
-    angle = 2.0 * np.pi * ((k[:, None] * k[None, :]) % QUARTER) / QUARTER
+    k = np.arange(128, dtype=np.int64)
+    angle = 2.0 * np.pi * ((k[:, None] * k[None, :]) % 128) / 128
     cosine, sine = np.cos(angle) / 32.0, np.sin(angle) / 32.0
     complex_dft = np.block([[cosine, -sine], [sine, cosine]])
-    turn = 2.0 * np.pi * np.arange(4)[:, None] * k[None, :] / GRID
+    turn = 2.0 * np.pi * np.arange(8)[:, None] * k[None, :] / GRID
     twiddle = np.concatenate([np.cos(turn), -np.sin(turn)]).astype(np.float32)
     return split_table(real_dft), split_table(complex_dft), twiddle
 
@@ -122,6 +122,16 @@
     ]
 
 
+def radix_eight(items):
+    even, odd = radix_four(items[0::2]), radix_four(items[1::2])
+    root = math.sqrt(0.5)
+    (r0, i0), (r1, i1), (r2, i2), (r3, i3) = odd
+    turned = [(r0, i0), (root * (r1 + i1), root * (i1 - r1)), (i2, -r2), (root * (i3 - r3), -root * (r3 + i3))]
+    return [(a[0] + b[0], a[1] + b[1]) for a, b in zip(even, turned)] + [
+        (a[0] - b[0], a[1] - b[1]) for a, b in zip(even, turned)
+    ]
+
+
 def times(item, cosine, sine):
     real, imag = item
     return real * cosine - imag * sine, real * sine + imag * cosine
@@ -143,13 +153,10 @@
     return source, receiver, rigidity, friction
 
 
-def wave_arrays(sort, j):
-    row = lax.broadcasted_iota(jnp.int32, (8, 128), 0)
-    lane = lax.broadcasted_iota(jnp.int32, (8, 128), 1)
-    half = row // 4 if sort == 2 else sort
-    kx = 4 * (lane + 128 * half) + row % 4
+def wave_arrays(kind, j):
+    kx = 8 * lax.broadcasted_iota(jnp.int32, (8, 128), 1) + lax.broadcasted_iota(jnp.int32, (8, 128), 0)
     signed = jnp.where(kx >= HALF, kx - GRID, kx)
-    ky = jnp.full((8, 128), -HALF, jnp.int32) if sort == 2 else 2 * j + row // 4
+    ky = jnp.full((8, 128), -HALF, jnp.int32) if kind == 2 else jnp.full((8, 128), 2 * j + kind, jnp.int32)
     x_wave, y_wave = signed.astype(F32), ky.astype(F32)
     magnitude = jnp.sqrt(x_wave * x_wave + y_wave * y_wave)
     bounded = jnp.maximum(magnitude, 1.0)
@@ -165,14 +172,14 @@
 
 def prepare(j, columns, wave_ref, grow_ref, fall_ref):
     source, receiver = columns[0], columns[1]
-    for sort in range(3):
-        arrays = wave_arrays(sort, j)
+    for kind in range(3):
+        arrays = wave_arrays(kind, j)
         for n, value in enumerate(arrays):
-            wave_ref[sort, n] = value
+            wave_ref[kind, n] = value
         for n, z in enumerate(source + receiver):
             exponent = arrays[0] * z
-            grow_ref[sort, n] = jnp.exp(exponent)
-            fall_ref[sort, n] = jnp.exp(-exponent)
+            grow_ref[kind, n] = jnp.exp(exponent)
+            fall_ref[kind, n] = jnp.exp(-exponent)
 
 
 def middle(
@@ -184,7 +191,6 @@
     out_ref,
     left_ref,
     spec_ref,
-    rim_ref,
     edge_ref,
     suffix_ref,
     trac_ref,
@@ -195,8 +201,8 @@
     source, receiver, rigidity, friction = columns
     keep_imag = jnp.where(j == 0, 0.0, 1.0).astype(F32)
     only_first = 1.0 - keep_imag
-    cosines = [twiddle_ref[a : a + 1, :] for a in range(4)]
-    sines = [twiddle_ref[4 + a : 5 + a, :] for a in range(4)]
+    cosines = [twiddle_ref[a : a + 1, :] for a in range(8)]
+    sines = [twiddle_ref[8 + a : 9 + a, :] for a in range(8)]
 
     loaded = [decode(got_ref[pl.ds(c, DEVICES, stride=4), :]) for c in range(4)]
     blocks = [[[None] * 8 for _ in range(4)] for _ in range(4)]
@@ -206,54 +212,33 @@
             for g in range(4):
                 blocks[c][g][outer] = group[g]
     for g in range(4):
-        whole = [
-            [jnp.concatenate([blocks[c][g][2 * x0], blocks[c][g][2 * x0 + 1]], axis=1) for x0 in range(4)]
-            for c in range(4)
+        kinds = [
+            [(blocks[0][g][o], blocks[1][g][o] * keep_imag) for o in range(8)],
+            [(blocks[2][g][o], blocks[3][g][o]) for o in range(8)],
+            [(blocks[1][g][o], jnp.zeros_like(blocks[1][g][o])) for o in range(8)],
         ]
-        kinds = [
-            [(whole[0][x0], whole[1][x0] * keep_imag) for x0 in range(4)],
-            [(whole[2][x0], whole[3][x0]) for x0 in range(4)],
-            [(whole[1][x0], jnp.zeros_like(whole[1][x0])) for x0 in range(4)],
-        ]
-        for p in range(3):
-            mixed = radix_four(kinds[p])
-            for k0 in range(4):
+        for kind in range(3):
+            mixed = radix_eight(kinds[kind])
+            for k0 in range(8):
                 real, imag = times(mixed[k0], cosines[k0], sines[k0]) if k0 else mixed[k0]
-                if p < 2:
-                    place = pl.ds(64 * g + 4 * p + k0, 8, stride=8)
-                else:
-                    place = pl.ds(256 + 32 * k0 + 8 * g, 8)
-                for t in range(2):
-                    left_ref.at[t][place, :] = real[:, 128 * t : 128 * t + 128]
-                    left_ref.at[2 + t][place, :] = imag[:, 128 * t : 128 * t + 128]
-    high, low = halves(jnp.concatenate([left_ref[t] for t in range(4)], axis=1))
+                place = pl.ds(64 * (4 * kind + g) + k0, 8, stride=8)
+                left_ref.at[0][place, :] = real
+                left_ref.at[1][place, :] = imag
+    high, low = halves(jnp.concatenate([left_ref[0], left_ref[1]], axis=1))
     spectra = dot(high, table_ref[0]) + dot(low, table_ref[0]) + dot(high, table_ref[1])
-    spectra = spectra.astype(BF16).astype(F32)
-    spec_ref[...] = spectra[:256]
-    for k0 in range(4):
-        for t in range(4):
-            rows = spectra[256 + 32 * k0 : 288 + 32 * k0, 128 * t : 128 * t + 128]
-            rim_ref.at[t // 2][pl.ds(4 * (t % 2) + k0, 32, stride=8), :] = rows
-
-    def unit(sort, row_weight, write):
-        wave, uu, uv, vv, odd_x, odd_y = [wave_ref[sort, n] for n in range(6)]
+    spec_ref[...] = spectra.astype(BF16).astype(F32)
+
+    def unit(kind, row_weight, write):
+        wave, uu, uv, vv, odd_x, odd_y = [wave_ref[kind, n] for n in range(6)]
 
         def fields(s):
-            picked = []
-            for q in range(2):
-                row = 8 * ((2 * (s % 2) + q) * 8 + s // 2)
-                for imag in range(2):
-                    if sort == 2:
-                        picked.append(rim_ref[imag, row : row + 8, :])
-                    else:
-                        start = 256 * imag + 128 * sort
-                        picked.append(spec_ref[row : row + 8, start : start + 128])
-            return picked
+            rows = [8 * (8 * (4 * kind + 2 * (s % 2) + q) + s // 2) for q in range(2)]
+            return [spec_ref[row : row + 8, 128 * n : 128 * n + 128] for row in rows for n in range(2)]
 
         zero = jnp.zeros((8, 128), F32)
         suffix, moment = [zero] * 4, [zero] * 4
         for s in reversed(range(S)):
-            decay = fall_ref[sort, s]
+            decay = fall_ref[kind, s]
             scaled = [decay * value for value in fields(s)]
             suffix = [a + b for a, b in zip(suffix, scaled)]
             moment = [a + source[s] * b for a, b in zip(moment, scaled)]
@@ -264,14 +249,14 @@
         total, total_moment = suffix, moment
         prefix, moment = [zero] * 4, [zero] * 4
         for s in range(S - 1):
-            growth = grow_ref[sort, s]
+            growth = grow_ref[kind, s]
             scaled = [growth * value for value in fields(s)]
             prefix = [a + b for a, b in zip(prefix, scaled)]
             moment = [a + source[s] * b for a, b in zip(moment, scaled)]
             if s % 2 == 0:
                 r = s // 2
                 z = receiver[r]
-                fall, rise = fall_ref[sort, S + r], grow_ref[sort, S + r]
+                fall, rise = fall_ref[kind, S + r], grow_ref[kind, S + r]
                 wave_fall, wave_rise = wave * fall, wave * rise
                 summed, slope = [], []
                 for n in range(4):
@@ -301,38 +286,34 @@
             edge_ref[r, n] = values[n]
 
     unit(2, only_first, write_edge)
-    kind = lax.broadcasted_iota(jnp.int32, (8, 128), 0) // 4
-    weight = jnp.where(kind == 0, 1.0 + keep_imag, 2.0).astype(F32)
-    pad = jnp.zeros((4, 128), F32)
-    for half in range(2):
+    for p in range(2):
 
         def write_main(r, values):
             for c in range(3):
-                edges = [
-                    jnp.concatenate([edge_ref[r, 2 * c + n, 4 * half : 4 * half + 4, :], pad], axis=0) for n in range(2)
-                ]
-                place = pl.ds(64 * c + r, 8, stride=8)
-                trac_ref.at[half][place, :] = values[2 * c] - edges[1]
-                trac_ref.at[2 + half][place, :] = -(values[2 * c + 1] + edges[0])
-
-        unit(half, weight, write_main)
-
-    high, low = halves(jnp.concatenate([trac_ref[t] for t in range(4)], axis=1))
+                real, imag = values[2 * c], values[2 * c + 1]
+                if p == 0:
+                    real, imag = real - edge_ref[r, 2 * c + 1], imag + edge_ref[r, 2 * c]
+                place = pl.ds(64 * (2 * c + p) + r, 8, stride=8)
+                trac_ref.at[0][place, :] = real
+                trac_ref.at[1][place, :] = -imag
+
+        unit(p, jnp.float32(2.0) if p else 1.0 + keep_imag, write_main)
+
+    high, low = halves(jnp.concatenate([trac_ref[0], trac_ref[1]], axis=1))
     turned = dot(high, table_ref[0]) + dot(low, table_ref[0]) + dot(high, table_ref[1])
     for c in range(3):
         fields = []
         for p in range(2):
             items = []
-            for k0 in range(4):
-                row = 64 * c + 32 * p + 8 * k0
-                item = (turned[row : row + 8, :256], turned[row : row + 8, 256:])
+            for k0 in range(8):
+                row = 64 * (2 * c + p) + 8 * k0
+                item = (turned[row : row + 8, :128], turned[row : row + 8, 128:])
                 items.append(times(item, cosines[k0], sines[k0]) if k0 else item)
-            mixed = radix_four(items)
+            mixed = radix_eight(items)
             fields.append([item[0] for item in mixed])
             fields.append([-item[1] for item in mixed])
         for outer in range(8):
-            cut = slice(128 * (outer % 2), 128 * (outer % 2) + 128)
-            group = swap_groups([fields[n][outer // 2][:, cut] for n in range(4)])
+            group = swap_groups([fields[n][outer] for n in range(4)])
             for inner in range(4):
                 w = 4 * outer + inner
                 out_ref[pl.ds(32 * w + c, 8, stride=4), :] = group[inner]
@@ -355,8 +336,18 @@
         out_ref[:, side * HALF : (side + 1) * HALF] = jnp.sqrt(first * first + second * second + 1.0) + third
 
 
-NEAR = (4, 3, 5, 2, 6, 1, 7, 0)
 MESH = pl.DeviceIdType.MESH
+
+
+def far_first():
+    places = [(z, y, x, c) for z in range(8) for y in range(4) for x in range(4) for c in range(2)][1:]
+
+    def rank(place):
+        z, y, x, c = place
+        hops = min(z, 8 - z) + min(y, 4 - y) + min(x, 4 - x)
+        return -hops, (z * 89 + y * 37 + x * 53 + c * 101) % 61, place
+
+    return sorted(places, key=rank)
 
 
 def fused(
@@ -384,7 +375,6 @@
     take_ref,
     left_ref,
     spec_ref,
-    rim_ref,
     edge_ref,
     suffix_ref,
     trac_ref,
@@ -395,7 +385,6 @@
     copy_sem,
     send_sem,
     take_sem,
-    ready_sem,
 ):
     w, d = lax.axis_index("wave"), lax.axis_index("depth")
     me = w * 8 + d
@@ -404,20 +393,16 @@
     x = 2 * high + low
     rings = [((z + n) % 8) * 4 for n in range(8)]
     cores = [core, 1 - core]
-
-    def greet(sem, pillar):
-        for n in range(1, 16):
-            if pillar:
-                other = 2 * low if n < 8 else 2 - 2 * low
-                place = (rings[n % 8] + other + core, d)
-            else:
-                side = 4 * high if (n // 2) % 2 == 0 else 4 - 4 * high
-                place = (4 * z + 2 * low + cores[n % 2], side + (y + n // 4) % 4)
-            pl.semaphore_signal(sem, 1, device_id=place, device_id_type=MESH)
+    lows = [((x + n) % 4 % 2) * 2 for n in range(4)]
+    highs = [((x + n) % 4 // 2) * 4 for n in range(4)]
+    columns_y = [(y + n) % 4 for n in range(4)]
+
+    def everyone(act):
+        for dz, dy, dx, dc in far_first():
+            act(rings[dz] + lows[dx] + cores[dc], highs[dx] + columns_y[dy])
 
     barrier = pltpu.get_barrier_semaphore()
-    greet(barrier, True)
-    greet(barrier, False)
+    everyone(lambda w_to, d_to: pl.semaphore_signal(barrier, 1, device_id=(w_to, d_to), device_id_type=MESH))
     pairs = (
         (slip_hbm, slip_ref),
         (mask_hbm, mask_ref),
@@ -435,34 +420,20 @@
         copy.wait()
     forward_rows(mask_ref, slip_ref, real_ref, rows_ref)
     sent_ref[...] = rows_ref[...].reshape(sent_ref.shape).astype(jnp.int32).astype(jnp.int16)
-    pl.semaphore_wait(barrier, 30)
-    greet(ready_sem, True)
-    pl.semaphore_wait(ready_sem, 15)
+    pl.semaphore_wait(barrier, DEVICES - 1)
 
     def exchange(source, target, number):
-        def send(w_base, d_to, skip):
-            for n in NEAR:
-                for c in (1, 0):
-                    if skip and n == 0 and c == 0:
-                        continue
-                    w_to = w_base + rings[n] + cores[c]
-                    pltpu.make_async_remote_copy(
-                        source.at[w_to * 8 + d_to],
-                        target.at[me],
-                        send_sem.at[number],
-                        take_sem.at[number],
-                        device_id=(w_to, d_to),
-                        device_id_type=MESH,
-                    ).start()
-
-        def sheet(n, carry):
-            order = (n + 11) % 16
-            y_to, x_to = (y + order // 4 + 2) % 4, (x + order + 2) % 4
-            send((x_to % 2) * 2, (x_to // 2) * 4 + y_to, False)
-            return carry
-
-        lax.fori_loop(0, 15, sheet, 0)
-        send(2 * low, d, True)
+        def send(w_to, d_to):
+            pltpu.make_async_remote_copy(
+                source.at[w_to * 8 + d_to],
+                target.at[me],
+                send_sem.at[number],
+                take_sem.at[number],
+                device_id=(w_to, d_to),
+                device_id_type=MESH,
+            ).start()
+
+        everyone(send)
         own = pltpu.make_async_copy(source.at[me], target.at[me], copy_sem.at[number])
         own.start()
         return own
@@ -489,7 +460,6 @@
         rows_ref,
         left_ref,
         spec_ref,
-        rim_ref,
         edge_ref,
         suffix_ref,
         trac_ref,
@@ -510,10 +480,11 @@
 
 def shards(slip_field, slip_mask, slice_layer, layer_material, materials):
     real_dft, complex_dft, twiddle = tables()
+    pin = functools.partial(pltpu.with_memory_space_constraint, memory_space=pltpu.HBM)
     result = pl.pallas_call(
         fused,
         out_shape=jax.ShapeDtypeStruct((32, GRID), F32),
-        in_specs=[spec(pl.ANY)] * 8,
+        in_specs=[spec(pltpu.HBM)] * 8,
         out_specs=spec(),
         scratch_shapes=[
             VMEM((2, 32), jnp.int32),
@@ -521,20 +492,19 @@
             SMEM((NZ,), jnp.int32),
             SMEM((16,), jnp.int32),
             SMEM((3, 8), F32),
-            VMEM((8, QUARTER), F32),
+            VMEM((16, 128), F32),
             VMEM((2, GRID, HALF), BF16),
-            VMEM((2, HALF, HALF), BF16),
+            VMEM((2, QUARTER, QUARTER), BF16),
             VMEM((4 * DEVICES, 128), F32),
             VMEM((DEVICES, 4, 128), jnp.int16),
             VMEM((DEVICES, 4, 128), jnp.int16),
             VMEM((DEVICES, 4, 128), BF16),
             VMEM((DEVICES, 4, 128), BF16),
-            VMEM((4, 384, 128), F32),
-            VMEM((256, 512), F32),
-            VMEM((2, 256, 128), F32),
+            VMEM((2, 768, 128), F32),
+            VMEM((768, 256), F32),
             VMEM((R, 6, 8, 128), F32),
             VMEM((R, 8, 8, 128), F32),
-            VMEM((4, 192, 128), F32),
+            VMEM((2, 384, 128), F32),
             VMEM((3, 6, 8, 128), F32),
             VMEM((3, S + R, 8, 128), F32),
             VMEM((3, S + R, 8, 128), F32),
@@ -542,19 +512,23 @@
             pltpu.SemaphoreType.DMA((2,)),
             pltpu.SemaphoreType.DMA((2,)),
             pltpu.SemaphoreType.DMA((2,)),
-            pltpu.SemaphoreType.REGULAR,
         ],
-        compiler_params=pltpu.CompilerParams(collective_id=0, has_side_effects=True),
+        compiler_params=pltpu.CompilerParams(collective_id=0, has_side_effects=True, vmem_limit_bytes=50000000),
         name="fused",
     )(
-        slip_mask.reshape((2, 32)),
-        slip_field.reshape((128, GRID)),
-        slice_layer,
-        layer_material,
-        materials,
-        twiddle,
-        real_dft,
-        complex_dft,
+        *map(
+            pin,
+            (
+                slip_mask.reshape((2, 32)),
+                slip_field.reshape((128, GRID)),
+                slice_layer,
+                layer_material,
+                materials,
+                jnp.asarray(twiddle),
+                jnp.asarray(real_dft),
+                jnp.asarray(complex_dft),
+            ),
+        )
     )
     return result.reshape((1, 32, GRID))
 

time: 39.7 us -> 36.9 us (0.929)
  Pallas kernels: 38 us -> 36.2 us
  local copies, waits for them, and re-layouts: 1.57 us -> 0.66 us
    pallas_call x1, Pallas kernels: 38 us -> 36.2 us  [shards(): pl.pallas_call(fused, out_shape=jax.ShapeDtypeStruct((32, GRID), F32), in...]
    unnamed x1, local copies, waits for them, and re-layouts: 1.57 us -> 0.66 us
where the time goes in v4:
time: 36.9 us; the launch traced here: 36.8 us
  Pallas kernels  36.2 us (98%)
  local copies, waits for them, and re-layouts  0.66 us (2%)
    pallas_call x1, Pallas kernels, shards(): pl.pallas_call(fused, out_shape=jax.ShapeDtypeStruct((32, GRID), F32), in...  36.2 us

profile of v4, /device:TPU:1, one launch (start us, length us, event | category | flops | bytes accessed | tf_op | source)
XLA Modules:
  0.0 36.8 jit_solution(397183407397252637)
XLA Ops:
  0.0 36.2 %fused.1 = f32[32,1024]{1,0:T(8,128)S(1)} custom-call(s32[2,32]{1,0:T(2,128)} %bitcast.5, bf16[128,1024]{1,0:T(8,128)(2,1)} %bitcast.4, s32[64]{0:T(128)} %slice_hbm.1, s32[16]{0:T(128)} %layer_hbm.1, f32[3,8]{1,0:T(4,128)} %material_hbm.1, f32[16,128]{1,0:T(8,128)} %constant.6.clone.twiddle_hbm, bf16[2,1024,512]{2,1,0:T(8,128)(2,1)} %constant.7.clone.real_hbm, ...), custom_call_target="tpu_custom_call" | custom-call | tf_op jit(solution)/shard_map/fused/pallas_call | solution.py:484
  36.2 0.7 %copy.10 = f32[1,32,1024]{2,1,0:T(8,128)} copy(f32[1,32,1024]{2,1,0:T(8,128)S(1)} %bitcast.3) | data formatting | bytes 262144

commit v5 on v4

--- a/solution.py
+++ b/solution.py
@@ -19,6 +19,8 @@
 DEVICES = 256
 LARGEST = 6.0 * GRID / 32.0
 CODE_SCALE = 32700.0 / LARGEST**0.25
+WIDEST = 2.0**20
+WIDE_SCALE = 32700.0 / WIDEST**0.125
 BF16 = jnp.bfloat16
 F32 = jnp.float32
 VMEM = pltpu.VMEM
@@ -106,6 +108,18 @@
     return jnp.where(value < 0.0, -code, code)
 
 
+def encode_wide(value):
+    size = jnp.maximum(jnp.abs(value), 1e-30)
+    code = jnp.exp2(jnp.log2(size) * 0.125 + math.log2(WIDE_SCALE)) + 0.5
+    return jnp.where(value < 0.0, -code, code)
+
+
+def decode_wide(code):
+    square = code * jnp.abs(code)
+    fourth = square * jnp.abs(square)
+    return fourth * jnp.abs(fourth) * (1.0 / WIDE_SCALE) ** 8
+
+
 def decode(code):
     return (code * jnp.abs(code)) * (code * code) * (1.0 / CODE_SCALE) ** 4
 
@@ -170,16 +184,24 @@
     return wave, along_x * along_x, cross, along_y * along_y, odd_x, odd_y
 
 
-def prepare(j, columns, wave_ref, grow_ref, fall_ref):
-    source, receiver = columns[0], columns[1]
+def prepare(j, columns, wave_ref, grow_ref, fall_ref, pair_ref):
+    source, receiver, rigidity, _ = columns
+    double = jnp.where(j == 0, 1.0, 2.0).astype(F32)
+    weights = [double, jnp.float32(2.0), 2.0 - double]
     for kind in range(3):
         arrays = wave_arrays(kind, j)
         for n, value in enumerate(arrays):
             wave_ref[kind, n] = value
-        for n, z in enumerate(source + receiver):
+        for n, z in enumerate(source):
             exponent = arrays[0] * z
             grow_ref[kind, n] = jnp.exp(exponent)
             fall_ref[kind, n] = jnp.exp(-exponent)
+        for r in range(R):
+            exponent = arrays[0] * receiver[r]
+            for n, sign in enumerate((-1.0, 1.0)):
+                weighted = (weights[kind] * rigidity[r]) * jnp.exp(sign * exponent)
+                pair_ref[kind, r, n] = weighted
+                pair_ref[kind, r, 2 + n] = arrays[0] * weighted
 
 
 def middle(
@@ -197,10 +219,10 @@
     wave_ref,
     grow_ref,
     fall_ref,
+    pair_ref,
 ):
     source, receiver, rigidity, friction = columns
     keep_imag = jnp.where(j == 0, 0.0, 1.0).astype(F32)
-    only_first = 1.0 - keep_imag
     cosines = [twiddle_ref[a : a + 1, :] for a in range(8)]
     sines = [twiddle_ref[8 + a : 9 + a, :] for a in range(8)]
 
@@ -228,8 +250,8 @@
     spectra = dot(high, table_ref[0]) + dot(low, table_ref[0]) + dot(high, table_ref[1])
     spec_ref[...] = spectra.astype(BF16).astype(F32)
 
-    def unit(kind, row_weight, write):
-        wave, uu, uv, vv, odd_x, odd_y = [wave_ref[kind, n] for n in range(6)]
+    def unit(kind, write):
+        uu, uv, vv, odd_x, odd_y = [wave_ref[kind, n] for n in range(1, 6)]
 
         def fields(s):
             rows = [8 * (8 * (4 * kind + 2 * (s % 2) + q) + s // 2) for q in range(2)]
@@ -246,8 +268,8 @@
                 for n in range(4):
                     suffix_ref[s // 2, n] = suffix[n]
                     suffix_ref[s // 2, 4 + n] = moment[n]
-        total, total_moment = suffix, moment
-        prefix, moment = [zero] * 4, [zero] * 4
+        twice = [a + a for a in suffix]
+        prefix = suffix
         for s in range(S - 1):
             growth = grow_ref[kind, s]
             scaled = [growth * value for value in fields(s)]
@@ -256,28 +278,24 @@
             if s % 2 == 0:
                 r = s // 2
                 z = receiver[r]
-                fall, rise = fall_ref[kind, S + r], grow_ref[kind, S + r]
-                wave_fall, wave_rise = wave * fall, wave * rise
+                fall, rise, wave_fall, wave_rise = [pair_ref[kind, r, n] for n in range(4)]
                 summed, slope = [], []
                 for n in range(4):
                     after, after_moment = suffix_ref[r, n], suffix_ref[r, 4 + n]
-                    summed.append(fall * (prefix[n] + total[n]) + rise * after)
+                    summed.append(fall * prefix[n] + rise * after)
                     slope.append(
-                        wave_fall * (z * (prefix[n] - total[n]) - (moment[n] + total_moment[n]))
-                        + wave_rise * (after_moment - z * after)
+                        wave_fall * (z * (prefix[n] - twice[n]) - moment[n]) + wave_rise * (after_moment - z * after)
                     )
-                weight = row_weight * rigidity[r]
-                tilt = weight * friction[r]
                 along = [a - b for a, b in zip(summed, slope)]
                 write(
                     r,
                     [
-                        weight * (summed[0] - uu * slope[0] - uv * slope[2]),
-                        weight * (summed[1] - uu * slope[1] - uv * slope[3]),
-                        weight * (summed[2] - uv * slope[0] - vv * slope[2]),
-                        weight * (summed[3] - uv * slope[1] - vv * slope[3]),
-                        -tilt * (odd_x * along[1] + odd_y * along[3]),
-                        tilt * (odd_x * along[0] + odd_y * along[2]),
+                        summed[0] - uu * slope[0] - uv * slope[2],
+                        summed[1] - uu * slope[1] - uv * slope[3],
+                        summed[2] - uv * slope[0] - vv * slope[2],
+                        summed[3] - uv * slope[1] - vv * slope[3],
+                        -friction[r] * (odd_x * along[1] + odd_y * along[3]),
+                        friction[r] * (odd_x * along[0] + odd_y * along[2]),
                     ],
                 )
 
@@ -285,7 +303,7 @@
         for n in range(6):
             edge_ref[r, n] = values[n]
 
-    unit(2, only_first, write_edge)
+    unit(2, write_edge)
     for p in range(2):
 
         def write_main(r, values):
@@ -297,7 +315,7 @@
                 trac_ref.at[0][place, :] = real
                 trac_ref.at[1][place, :] = -imag
 
-        unit(p, jnp.float32(2.0) if p else 1.0 + keep_imag, write_main)
+        unit(p, write_main)
 
     high, low = halves(jnp.concatenate([trac_ref[0], trac_ref[1]], axis=1))
     turned = dot(high, table_ref[0]) + dot(low, table_ref[0]) + dot(high, table_ref[1])
@@ -316,11 +334,11 @@
             group = swap_groups([fields[n][outer] for n in range(4)])
             for inner in range(4):
                 w = 4 * outer + inner
-                out_ref[pl.ds(32 * w + c, 8, stride=4), :] = group[inner]
+                out_ref[pl.ds(32 * w + c, 8, stride=4), :] = encode_wide(group[inner])
 
 
 def inverse_rows(table_ref, got_ref, out_ref):
-    flipped = [got_ref[pl.ds(c, DEVICES, stride=4), :].T for c in range(3)]
+    flipped = [decode_wide(got_ref[pl.ds(c, DEVICES, stride=4), :]).T for c in range(3)]
     parts = []
     for parity in range(2):
         rows = []
@@ -328,9 +346,11 @@
             real = flipped[c][64 * parity : 64 * parity + 32]
             imag = flipped[c][64 * parity + 32 : 64 * parity + 64]
             rows.append(jnp.concatenate([real, imag], axis=1))
-        whole = jnp.concatenate(rows, axis=0).astype(BF16)
+        high, low = halves(jnp.concatenate(rows, axis=0))
         part = slice(parity * HALF, (parity + 1) * HALF)
-        parts.append(dot(whole, table_ref[0, part]) + dot(whole, table_ref[1, part]))
+        parts.append(
+            dot(high, table_ref[0, part]) + dot(low, table_ref[0, part]) + dot(high, table_ref[1, part])
+        )
     for side, stress in enumerate((parts[0] + parts[1], parts[0] - parts[1])):
         first, second, third = stress[0:32], stress[32:64], stress[64:96]
         out_ref[:, side * HALF : (side + 1) * HALF] = jnp.sqrt(first * first + second * second + 1.0) + third
@@ -381,6 +401,7 @@
     wave_ref,
     grow_ref,
     fall_ref,
+    pair_ref,
     input_sem,
     copy_sem,
     send_sem,
@@ -397,12 +418,16 @@
     highs = [((x + n) % 4 // 2) * 4 for n in range(4)]
     columns_y = [(y + n) % 4 for n in range(4)]
 
-    def everyone(act):
-        for dz, dy, dx, dc in far_first():
+    def everyone(act, part=slice(None)):
+        for dz, dy, dx, dc in far_first()[part]:
             act(rings[dz] + lows[dx] + cores[dc], highs[dx] + columns_y[dy])
 
     barrier = pltpu.get_barrier_semaphore()
-    everyone(lambda w_to, d_to: pl.semaphore_signal(barrier, 1, device_id=(w_to, d_to), device_id_type=MESH))
+
+    def greet(w_to, d_to):
+        pl.semaphore_signal(barrier, 1, device_id=(w_to, d_to), device_id_type=MESH)
+
+    everyone(greet, slice(0, 64))
     pairs = (
         (slip_hbm, slip_ref),
         (mask_hbm, mask_ref),
@@ -416,6 +441,7 @@
     copies = [pltpu.make_async_copy(a, b, input_sem.at[n]) for n, (a, b) in enumerate(pairs)]
     for copy in copies:
         copy.start()
+    everyone(greet, slice(64, None))
     for copy in copies[:3]:
         copy.wait()
     forward_rows(mask_ref, slip_ref, real_ref, rows_ref)
@@ -438,18 +464,21 @@
         own.start()
         return own
 
-    def finish(own, source, target, number):
+    most = pl.ds(0, DEVICES - 1)
+
+    def arrived(own, source, target, number):
         own.wait()
-        most = pl.ds(0, DEVICES - 1)
+        pltpu.make_async_copy(source.at[most], target.at[most], take_sem.at[number]).wait()
+
+    def left(source, target, number):
         pltpu.make_async_copy(source.at[most], target.at[most], send_sem.at[number]).wait()
-        pltpu.make_async_copy(source.at[most], target.at[most], take_sem.at[number]).wait()
 
     own = exchange(sent_ref, got_ref, 0)
     for copy in copies[3:]:
         copy.wait()
     columns = depths(slice_ref, layer_ref, material_ref)
-    prepare(me, columns, wave_ref, grow_ref, fall_ref)
-    finish(own, sent_ref, got_ref, 0)
+    prepare(me, columns, wave_ref, grow_ref, fall_ref, pair_ref)
+    arrived(own, sent_ref, got_ref, 0)
     rows_ref[...] = got_ref[...].astype(jnp.int32).astype(F32).reshape(rows_ref.shape)
     middle(
         me,
@@ -466,12 +495,15 @@
         wave_ref,
         grow_ref,
         fall_ref,
+        pair_ref,
     )
-    send_ref[...] = rows_ref[...].reshape(send_ref.shape).astype(BF16)
+    send_ref[...] = rows_ref[...].reshape(send_ref.shape).astype(jnp.int32).astype(jnp.int16)
     own = exchange(send_ref, take_ref, 1)
-    finish(own, send_ref, take_ref, 1)
-    rows_ref[...] = take_ref[...].astype(F32).reshape(rows_ref.shape)
+    arrived(own, send_ref, take_ref, 1)
+    rows_ref[...] = take_ref[...].astype(jnp.int32).astype(F32).reshape(rows_ref.shape)
     inverse_rows(real_ref, rows_ref, out_ref)
+    left(sent_ref, got_ref, 0)
+    left(send_ref, take_ref, 1)
 
 
 def spec(space=VMEM):
@@ -498,16 +530,17 @@
             VMEM((4 * DEVICES, 128), F32),
             VMEM((DEVICES, 4, 128), jnp.int16),
             VMEM((DEVICES, 4, 128), jnp.int16),
-            VMEM((DEVICES, 4, 128), BF16),
-            VMEM((DEVICES, 4, 128), BF16),
+            VMEM((DEVICES, 4, 128), jnp.int16),
+            VMEM((DEVICES, 4, 128), jnp.int16),
             VMEM((2, 768, 128), F32),
             VMEM((768, 256), F32),
             VMEM((R, 6, 8, 128), F32),
             VMEM((R, 8, 8, 128), F32),
             VMEM((2, 384, 128), F32),
             VMEM((3, 6, 8, 128), F32),
-            VMEM((3, S + R, 8, 128), F32),
-            VMEM((3, S + R, 8, 128), F32),
+            VMEM((3, S, 8, 128), F32),
+            VMEM((3, S, 8, 128), F32),
+            VMEM((3, R, 4, 8, 128), F32),
             pltpu.SemaphoreType.DMA((8,)),
             pltpu.SemaphoreType.DMA((2,)),
             pltpu.SemaphoreType.DMA((2,)),

time: 36.9 us -> 37 us (level)
  no operation moved by 1% of the time
where the time goes in v5:
time: 37 us; the launch traced here: 36.9 us
  Pallas kernels  36.3 us (98%)
  local copies, waits for them, and re-layouts  0.66 us (2%)
    pallas_call x1, Pallas kernels, shards(): pl.pallas_call(fused, out_shape=jax.ShapeDtypeStruct((32, GRID), F32), in...  36.3 us

profile of v5, /device:TPU:1, one launch (start us, length us, event | category | flops | bytes accessed | tf_op | source)
XLA Modules:
  0.0 36.9 jit_solution(7882705095278251199)
XLA Ops:
  0.0 36.3 %fused.1 = f32[32,1024]{1,0:T(8,128)S(1)} custom-call(s32[2,32]{1,0:T(2,128)} %bitcast.5, bf16[128,1024]{1,0:T(8,128)(2,1)} %bitcast.4, s32[64]{0:T(128)} %slice_hbm.1, s32[16]{0:T(128)} %layer_hbm.1, f32[3,8]{1,0:T(4,128)} %material_hbm.1, f32[16,128]{1,0:T(8,128)} %constant.6.clone.twiddle_hbm, bf16[2,1024,512]{2,1,0:T(8,128)(2,1)} %constant.7.clone.real_hbm, ...), custom_call_target="tpu_custom_call" | custom-call | tf_op jit(solution)/shard_map/fused/pallas_call | solution.py:516
  36.3 0.7 %copy.10 = f32[1,32,1024]{2,1,0:T(8,128)} copy(f32[1,32,1024]{2,1,0:T(8,128)S(1)} %bitcast.3) | data formatting | bytes 262144

commit v6 on v5

--- a/solution.py
+++ b/solution.py
@@ -356,7 +356,7 @@
         out_ref[:, side * HALF : (side + 1) * HALF] = jnp.sqrt(first * first + second * second + 1.0) + third
 
 
-MESH = pl.DeviceIdType.MESH
+LOGICAL = pl.DeviceIdType.LOGICAL
 
 
 def far_first():
@@ -417,15 +417,17 @@
     lows = [((x + n) % 4 % 2) * 2 for n in range(4)]
     highs = [((x + n) % 4 // 2) * 4 for n in range(4)]
     columns_y = [(y + n) % 4 for n in range(4)]
+    depth_first = [[8 * (ring + c) for c in cores] for ring in rings]
+    sheets = [[8 * low_to + high_to + y_to for low_to, high_to in zip(lows, highs)] for y_to in columns_y]
 
     def everyone(act, part=slice(None)):
         for dz, dy, dx, dc in far_first()[part]:
-            act(rings[dz] + lows[dx] + cores[dc], highs[dx] + columns_y[dy])
+            act(depth_first[dz][dc] + sheets[dy][dx])
 
     barrier = pltpu.get_barrier_semaphore()
 
-    def greet(w_to, d_to):
-        pl.semaphore_signal(barrier, 1, device_id=(w_to, d_to), device_id_type=MESH)
+    def greet(to):
+        pl.semaphore_signal(barrier, 1, device_id=to, device_id_type=LOGICAL)
 
     everyone(greet, slice(0, 64))
     pairs = (
@@ -449,14 +451,14 @@
     pl.semaphore_wait(barrier, DEVICES - 1)
 
     def exchange(source, target, number):
-        def send(w_to, d_to):
+        def send(to):
             pltpu.make_async_remote_copy(
-                source.at[w_to * 8 + d_to],
+                source.at[to],
                 target.at[me],
                 send_sem.at[number],
                 take_sem.at[number],
-                device_id=(w_to, d_to),
-                device_id_type=MESH,
+                device_id=to,
+                device_id_type=LOGICAL,
             ).start()
 
         everyone(send)

time: 37 us -> 36.9 us (level)
  no operation moved by 1% of the time
where the time goes in v6:
time: 36.9 us; the launch traced here: 36.8 us
  Pallas kernels  36.1 us (98%)
  local copies, waits for them, and re-layouts  0.66 us (2%)
    pallas_call x1, Pallas kernels, shards(): pl.pallas_call(fused, out_shape=jax.ShapeDtypeStruct((32, GRID), F32), in...  36.1 us

profile of v6, /device:TPU:1, one launch (start us, length us, event | category | flops | bytes accessed | tf_op | source)
XLA Modules:
  0.0 36.8 jit_solution(16895218086127372826)
XLA Ops:
  0.0 36.1 %fused.1 = f32[32,1024]{1,0:T(8,128)S(1)} custom-call(s32[2,32]{1,0:T(2,128)} %bitcast.5, bf16[128,1024]{1,0:T(8,128)(2,1)} %bitcast.4, s32[64]{0:T(128)} %slice_hbm.1, s32[16]{0:T(128)} %layer_hbm.1, f32[3,8]{1,0:T(4,128)} %material_hbm.1, f32[16,128]{1,0:T(8,128)} %constant.6.clone.twiddle_hbm, bf16[2,1024,512]{2,1,0:T(8,128)(2,1)} %constant.7.clone.real_hbm, ...), custom_call_target="tpu_custom_call" | custom-call | tf_op jit(solution)/shard_map/fused/pallas_call | solution.py:518
  36.1 0.7 %copy.10 = f32[1,32,1024]{2,1,0:T(8,128)} copy(f32[1,32,1024]{2,1,0:T(8,128)S(1)} %bitcast.3) | data formatting | bytes 262144
